TPU v7x, 512 devices: a whole 4x8x8 slice. The times are simulated.
512 devices in a mesh: tile: 128 (over z, y, core), filt: 2 (over x_hi), mc: 2 (over x_lo).
Axes of the slice: x: 4 (x_hi: 2, x_lo: 2; x = x_hi * 2 + x_lo), y: 8, z: 8, core: 2. Of those that a mesh axis runs over, the one named last changes fastest.
Arguments:
- sky_mean: float32 [128, 6, 256, 256], P('tile', 'filt'), may hold values from -6 to 6
- sky_log_scale: float32 [128, 6, 256, 256], P('tile', 'filt'), may hold values from -2.5 to -0.5
- noise_draw: bfloat16 [2, 128, 6, 256, 256], P('mc', 'tile', 'filt'), may hold values from -5 to 5
- observed: bfloat16 [128, 6, 256, 256], P('tile', 'filt'), may hold values from -6 to 6
- inv_var: bfloat16 [128, 6, 256, 256], P('tile', 'filt'), may hold values from 0.5 to 4
- intersections: int32 [128, 6, 3, 9], replicated, may hold values from -128 to 128, as said below
- counts: int32 [128, 6], replicated, may hold values from 1 to 3, as said below
- kernels: float32 [8, 2, 25], replicated, may hold values from 0 to 0.08
- psf_coeffs: bfloat16 [128, 6, 6, 3], replicated, may hold values from -0.5 to 1
- prior_prec: float32 [6, 6], replicated, as said below
Outputs:
- grad_mu: float32 [128, 6, 256, 256], P('tile', 'filt')
- grad_rho: float32 [128, 6, 256, 256], P('tile', 'filt')
Inputs may be any that keep to these rules, and one draw needn't show every extreme that they name: `intersections`: for tile t and filter f the first counts[t, f] slots name distinct exposures within 2 of t; later slots hold values in the same ranges and are not used. Offsets lie in -128 .. 128 and kernel indices in 0 .. 7. counts[t, f] never exceeds the number of exposures within 2 of tile t. `prior_prec`: Symmetric; each diagonal entry exceeds the sum of the magnitudes of the other entries of its row.
All inputs are finite; a program needn't handle non-finite values.
Results may differ from a plain program's by a relative error of at most 0.00086.
Values may be sent and summed in bfloat16 or wider, within the bound.
A program may use at most 64 MiB of HBM per device.

v0:
```python
import jax
import jax.numpy as jnp
from jax import lax
from jax.sharding import PartitionSpec as P

NB = 6
K = 3
REACH = 2


def shifted(x, axis, by):
    length = lax.axis_size(axis)
    pairs = [(i, i + by) for i in range(length) if 0 <= i + by < length]
    return lax.ppermute(x, axis, pairs)


def build_padded(kernels, tile_side):
    tap_count = kernels.shape[2]
    half_span = (tap_count - 1) // 2
    offsets = jnp.arange(tile_side)[:, None] - jnp.arange(tile_side)[None, :] + half_span
    summed = jnp.zeros((kernels.shape[0], 2, tile_side, tile_side), jnp.float32)
    for tap_id in range(tap_count):
        summed = summed + kernels[:, :, tap_id][:, :, None, None] * (offsets == tap_id).astype(
            jnp.float32
        )
    return jnp.pad(summed.astype(jnp.bfloat16), ((0, 0), (0, 0), (tile_side, tile_side), (0, 0)))


def shifted_basis(basis_pad, basis_id, side_id, offset, tile_side):
    starts = (basis_id, jnp.int32(side_id), tile_side - offset, jnp.int32(0))
    return lax.dynamic_slice(basis_pad, starts, (1, 1, tile_side, tile_side))[0, 0]


def weight_map(coeff_row, tile_side):
    centred = (2.0 * jnp.arange(tile_side, dtype=jnp.float32) + 1.0 - tile_side) / tile_side
    coeff_f = coeff_row.astype(jnp.float32)
    return coeff_f[0] + coeff_f[1] * centred[:, None] + coeff_f[2] * centred[None, :]


def contribution(basis_pad, image, slot_entry, coeff_rows, tile_side):
    summed = jnp.zeros((tile_side, tile_side), jnp.float32)
    for component in range(NB):
        basis_id = slot_entry[3 + component]
        rows_matrix = shifted_basis(basis_pad, basis_id, 0, slot_entry[1], tile_side)
        cols_matrix = shifted_basis(basis_pad, basis_id, 1, slot_entry[2], tile_side)
        half_blur = jnp.dot(rows_matrix, image, preferred_element_type=jnp.float32).astype(
            jnp.bfloat16
        )
        blurred = lax.dot_general(
            half_blur, cols_matrix, (((1,), (1,)), ((), ())), preferred_element_type=jnp.float32
        )
        summed = summed + weight_map(coeff_rows[component], tile_side) * blurred
    return summed.astype(jnp.bfloat16)


def adjoint_term(basis_pad, resid_img, slot_entry, coeff_rows, tile_side):
    summed = jnp.zeros((tile_side, tile_side), jnp.float32)
    for component in range(NB):
        basis_id = slot_entry[3 + component]
        rows_matrix = shifted_basis(basis_pad, basis_id, 0, slot_entry[1], tile_side)
        cols_matrix = shifted_basis(basis_pad, basis_id, 1, slot_entry[2], tile_side)
        weighted = (
            weight_map(coeff_rows[component], tile_side) * resid_img.astype(jnp.float32)
        ).astype(jnp.bfloat16)
        back_half = lax.dot_general(
            rows_matrix, weighted, (((0,), (0,)), ((), ())), preferred_element_type=jnp.float32
        ).astype(jnp.bfloat16)
        summed = summed + jnp.dot(back_half, cols_matrix, preferred_element_type=jnp.float32)
    return summed


def body(
    sky_mean,
    sky_log_scale,
    noise_draw,
    observed,
    inv_var,
    intersections,
    counts,
    kernels,
    psf_coeffs,
    prior_prec,
):
    tile_side = sky_mean.shape[2]
    local_filters = sky_mean.shape[1]
    slot_fields = intersections.shape[3]
    window_len = 2 * REACH + 1
    neighbour_moves = [amount for amount in range(-REACH, REACH + 1) if amount != 0]
    tile_here = lax.axis_index("tile")
    first_filter = lax.axis_index("filt") * local_filters
    basis_pad = build_padded(kernels, tile_side)
    scale_map = jnp.exp(sky_log_scale[0])
    eps_float = noise_draw[0, 0].astype(jnp.float32)
    sample = sky_mean[0] + scale_map * eps_float
    sample_b = sample.astype(jnp.bfloat16)
    my_slots = lax.dynamic_slice(
        intersections,
        (tile_here, first_filter, jnp.int32(0), jnp.int32(0)),
        (1, local_filters, K, slot_fields),
    )[0]
    my_counts = lax.dynamic_slice(counts, (tile_here, first_filter), (1, local_filters))[0]
    my_coeffs = lax.dynamic_slice_in_dim(psf_coeffs, first_filter, local_filters, 1)
    zero_image = jnp.zeros((tile_side, tile_side), jnp.float32)
    outgoing_rows = []
    for filt_id in range(local_filters):

        def place_slot(slot_id, buffer):
            slot_entry = my_slots[filt_id, slot_id]
            exposure = slot_entry[0]
            contrib = contribution(
                basis_pad, sample_b[filt_id], slot_entry, my_coeffs[exposure, filt_id], tile_side
            )
            return lax.dynamic_update_index_in_dim(buffer, contrib, exposure - tile_here + REACH, 0)

        empty_rows = jnp.zeros((window_len, tile_side, tile_side), jnp.bfloat16)
        outgoing_rows.append(lax.fori_loop(0, my_counts[filt_id], place_slot, empty_rows))
    outgoing = jnp.stack(outgoing_rows, 1)
    predicted = outgoing[REACH].astype(jnp.float32)
    for amount in neighbour_moves:
        arrived = shifted(outgoing[REACH + amount], "tile", amount)
        predicted = predicted + arrived.astype(jnp.float32)
    residual = (
        inv_var[0].astype(jnp.float32) * (observed[0].astype(jnp.float32) - predicted)
    ).astype(jnp.bfloat16)
    near_resid = [residual] * window_len
    for amount in neighbour_moves:
        near_resid[REACH + amount] = shifted(residual, "tile", -amount)
    near_stack = jnp.stack(near_resid, 0)
    grad_rows = []
    for filt_id in range(local_filters):

        def add_back(slot_id, running):
            slot_entry = my_slots[filt_id, slot_id]
            exposure = slot_entry[0]
            resid_img = lax.dynamic_index_in_dim(
                near_stack, exposure - tile_here + REACH, 0, keepdims=False
            )[filt_id]
            return running + adjoint_term(
                basis_pad, resid_img, slot_entry, my_coeffs[exposure, filt_id], tile_side
            )

        grad_rows.append(lax.fori_loop(0, my_counts[filt_id], add_back, zero_image))
    data_grad = jnp.stack(grad_rows, 0)
    every_filter = lax.all_gather(sample, "filt", axis=0, tiled=True)
    prec_rows = lax.dynamic_slice_in_dim(prior_prec, first_filter, local_filters, 0)
    prior_grad = jnp.einsum("fg,gij->fij", prec_rows, every_filter, precision=lax.Precision.HIGHEST)
    sample_grad = data_grad - prior_grad
    samples = lax.axis_size("mc")
    summed = lax.psum((sample_grad, sample_grad * scale_map * eps_float), "mc")
    mean_sum = summed[0]
    scale_sum = summed[1]
    return ((mean_sum / samples)[None], (scale_sum / samples + 1.0)[None])


def solution(mesh):
    placed = (
        P("tile", "filt", None, None),
        P("tile", "filt", None, None),
        P("mc", "tile", "filt", None, None),
        P("tile", "filt", None, None),
        P("tile", "filt", None, None),
        P(),
        P(),
        P(),
        P(),
        P(),
    )
    return jax.shard_map(
        body,
        mesh=mesh,
        in_specs=placed,
        out_specs=(P("tile", "filt", None, None), P("tile", "filt", None, None)),
        check_vma=False,
    )
```

profile of v0, /device:TPU:1, one launch (start us, length us, event | category | flops | bytes accessed | tf_op | source)
XLA Modules:
  0.0 934.9 jit_solution(9243033571776299060)
XLA Ops:
  7.3 1.6 fusion.788
  37.9 2.7 fusion.744
  40.9 10.3 %add_convert_fusion = bf16[8,2,256,256]{3,2,1,0:T(8,128)(2,1)S(1)} fusion(f32[256,256]{1,0:T(8,128)S(1)} %copy-done.12, f32[8,2]{1,0:T(8,128)S(1)} %copy-done.33, f32[256,256]{1,0:T(8,128)S(1)} %copy-done.11, f32[8,2]{1,0:T(8,128)S(1)} %copy-done.32, f32[256,256]{1,0:T(8,128)S(1)} %copy-done.10, f32[8,2]{1,0:T(8,128)S(1)} %copy-done.21, ...), kind=kLoop, calls=%fused_computation.615 | loop fusion | flops 52428800 | bytes 8652352 | tf_op jit(solution)/shard_map/convert_element_type | solution.py:26
  51.3 3.4 pad.4
  54.7 78.7 %while.90 = (s32[]{:T(128)}, bf16[5,256,256]{2,1,0:T(8,128)(2,1)S(1)}, s32[]{:T(128)}, s32[3,3,9]{2,1,0:T(4,128)}, bf16[128,3,6,3]{0,3,2,1:T(4,128)(2,1)S(1)}, /...) while((s32[]{:T(128)}, ...), condition=%wide.region_1.2_spmd, body=%wide.region_0.1_spmd.sunk | while | flops 404236864 | bytes 5150511 | solution.py:116
  134.6 41.0 %while.91 = (s32[]{:T(128)}, bf16[5,256,256]{2,1,0:T(8,128)(2,1)}, s32[]{:T(128)}, s32[3,3,9]{2,1,0:T(4,128)}, bf16[128,3,6,3]{0,3,2,1:T(4,128)(2,1)S(1)}, /*ind...) while((s32[]{:T(128)}, bf16[5,256,256]{2,1,0:T(8,128)(2,1)}, ...), condition=%wide.region_3.4_spmd, body=%wide.region_2.3_spmd.sunk | while | flops 404236864 | bytes 5150511 | solution.py:116
  173.0 2.0 fusion.1053
  175.7 80.0 %while.92 = (s32[]{:T(128)}, bf16[5,256,256]{2,1,0:T(8,128)(2,1)S(1)}, s32[]{:T(128)}, s32[3,3,9]{2,1,0:T(4,128)}, bf16[128,3,6,3]{0,3,2,1:T(4,128)(2,1)S(1)}, /...) while((s32[]{:T(128)}, ...), condition=%wide.region_5.6_spmd, body=%wide.region_4.5_spmd.sunk | while | flops 404236864 | bytes 5150511 | solution.py:116
  255.7 1.6 pad_maximum_fusion
  258.7 8.1 collective-permute-start.1
  266.8 40.1 %collective-permute-start.2 = (bf16[3,256,256]{2,1,0:T(8,128)(2,1)S(1)}, bf16[3,256,256]{2,1,0:T(8,128)(2,1)S(1)}, u32[]{:S(2)}, u32[]{:S(2)}) collective-permute-start(bf16[3,256,256]{2,1,0:T(8,128)(2,1)S(1)} %get-tuple-element.1578), channel_id=1, source_target_pairs={{0,4},{4,8},{8,12},{12,16},{16,20},{20,24},{24,28},{28,32},{32,36}... | collective-permute-start | bytes 1179656 | tf_op jit(solution)/shard_map/ppermute | solution.py:14
  306.9 3.7 collective-permute-start.3
  310.6 2.1 collective-permute-done.1
  312.9 7.2 collective-permute-done.3
  320.4 4.6 collective-permute-start.4
  325.0 2.5 collective-permute-start.5
  328.6 1.9 collective-permute-start.6
  334.2 3.1 collective-permute-done.5
  337.4 33.5 %collective-permute-done.6 = bf16[3,256,256]{2,1,0:T(8,128)(2,1)S(1)} collective-permute-done((bf16[3,256,256]{2,1,0:T(8,128)(2,1)S(1)}, bf16[3,256,256]{2,1,0:T(8,128)(2,1)S(1)}, u32[]{:S(2)}, u32[]{:S(2)}) %collective-permute-start.6) | collective-permute-done | bytes 393248 | tf_op jit(solution)/shard_map/ppermute | solution.py:14
  371.0 8.5 collective-permute-done.7
  379.5 80.7 %while.93 = (s32[]{:T(128)}, f32[256,256]{1,0:T(8,128)S(1)}, s32[]{:T(128)}, s32[3,3,9]{2,1,0:T(4,128)}, bf16[8,2,768,256]{3,2,1,0:T(8,128)(2,1)}, /*index=5*/bf...) while((s32[]{:T(128)}, f32[256,256]{1,0:T(8,128)S(1)}, ...), condition=%wide.region_7.8_spmd, body=%wide.region_6.7_spmd.sunk | while | flops 405023296 | bytes 5546287 | solution.py:142
  396.0 1.4 convolution_add_fusion.27
  407.0 1.4 convolution_add_fusion.29
  412.7 1.4 convolution_add_fusion.30
  418.1 1.4 fusion.1118
  436.1 1.4 convolution_add_fusion.27
  452.8 1.4 convolution_add_fusion.30
  458.2 1.4 fusion.1118
  460.9 41.2 %while.94 = (s32[]{:T(128)}, f32[256,256]{1,0:T(8,128)}, s32[]{:T(128)}, s32[3,3,9]{2,1,0:T(4,128)}, bf16[8,2,768,256]{3,2,1,0:T(8,128)(2,1)}, /*index=5*/bf16[1...) while((s32[]{:T(128)}, f32[256,256]{1,0:T(8,128)}, ...), condition=%wide.region_9.10_spmd, body=%wide.region_8.9_spmd.sunk | while | flops 405023296 | bytes 5549359 | solution.py:142
  477.7 1.4 convolution_add_fusion.31
  483.4 1.4 convolution_add_fusion.32
  488.7 1.4 convolution_add_fusion.33
  494.3 1.4 convolution_add_fusion.34
  499.3 2.2 fusion.1149
  502.2 81.5 %while.95 = (s32[]{:T(128)}, f32[256,256]{1,0:T(8,128)S(1)}, s32[]{:T(128)}, s32[3,3,9]{2,1,0:T(4,128)}, bf16[8,2,768,256]{3,2,1,0:T(8,128)(2,1)}, /*index=5*/bf...) while((s32[]{:T(128)}, f32[256,256]{1,0:T(8,128)S(1)}, ...), condition=%wide.region_11.12_spmd, body=%wide.region_10.11_spmd.sunk | while | flops 405023296 | bytes 5549359 | solution.py:142
  519.7 1.4 convolution_add_fusion.35
  525.5 1.4 convolution_add_fusion.36
  530.6 1.4 convolution_add_fusion.37
  536.0 1.4 convolution_add_fusion.38
  541.2 1.4 fusion.1180
  560.2 1.4 convolution_add_fusion.35
  565.9 1.4 convolution_add_fusion.36
  571.1 1.4 convolution_add_fusion.37
  576.5 1.4 convolution_add_fusion.38
  581.7 1.4 fusion.1180
  585.2 7.0 convert_multiply_fusion.18
  592.2 332.0 %all-reduce.4.cloned.1.call-done = (f32[3,256,256]{2,0,1:T(4,128)}, f32[3,256,256]{2,0,1:T(4,128)}) async-done(((f32[3,256,256]{2,0,1:T(4,128)}, f32[3,256,256]{2,0,1:T(4,128)}), (f32[3,256,256]{2,0,1:T(4,128)}, f32[3,256,256]{2,0,1:T(4,128)})) %all-reduce.4.cloned.1.call-update) | async-done | bytes 1572880 | tf_op jit(solution)/shard_map/psum | solution.py:149
  924.2 1.5 multiply_bitcast_fusion
  (398 shorter events, 163.9 us)
Async XLA Ops:
  7.2 28.8 %copy-start = (s32[128,6,3,9]{0,2,3,1:T(4,128)S(1)}, s32[128,6,3,9]{0,2,3,1:T(4,128)}, u32[]{:S(2)}) copy-start(s32[128,6,3,9]{0,2,3,1:T(4,128)} %param.27) | copy-start | bytes 248836
  7.2 29.6 %copy-start.39 = (s32[128,6]{0,1:T(8,128)S(1)}, s32[128,6]{0,1:T(8,128)}, u32[]{:S(2)}) copy-start(s32[128,6]{0,1:T(8,128)} %param.28) | copy-start | bytes 9220
  7.2 30.5 %copy-start.38 = (bf16[128,6,6,3]{0,3,2,1:T(4,128)(2,1)S(1)}, bf16[128,6,6,3]{0,3,2,1:T(4,128)(2,1)}, u32[]{:S(2)}) copy-start(bf16[128,6,6,3]{0,3,2,1:T(4,128)(2,1)} %param.30) | copy-start | bytes 82948
  7.2 30.5 %copy-start.14 = (f32[1,3,256,256]{3,2,1,0:T(8,128)S(1)}, f32[1,3,256,256]{3,2,1,0:T(8,128)}, u32[]{:S(2)}) copy-start(f32[1,3,256,256]{3,2,1,0:T(8,128)} %param.23) | copy-start | bytes 2359300
  7.2 578.0 %all-gather.2.cloned.1.call-start = ((), (), s32[]{:S(2)}) async-start(), calls=%async_computation | async-start | bytes 2359296 | tf_op jit(solution)/shard_map/all_gather | solution.py:144
  10.0 27.9 %copy-start.3 = (bf16[1,1,3,256,256]{4,3,2,1,0:T(8,128)(2,1)S(1)}, bf16[1,1,3,256,256]{4,3,2,1,0:T(8,128)(2,1)}, u32[]{:S(2)}) copy-start(bf16[1,1,3,256,256]{4,3,2,1,0:T(8,128)(2,1)} %param.24) | copy-start | bytes 1179652
  36.8 3.9 copy-start.4
  36.8 3.9 copy-start.5
  36.8 3.9 copy-start.6
  36.8 3.9 copy-start.7
  36.8 3.9 copy-start.8
  36.8 3.9 copy-start.9
  36.8 3.9 copy-start.10
  36.8 3.9 copy-start.11
  36.8 3.9 copy-start.12
  36.8 3.9 copy-start.17
  36.9 3.9 copy-start.18
  36.9 3.9 copy-start.19
  36.9 3.9 copy-start.20
  36.9 3.9 copy-start.21
  36.9 3.9 copy-start.22
  36.9 3.9 copy-start.23
  36.9 3.9 copy-start.24
  36.9 3.9 copy-start.25
  36.9 3.9 copy-start.26
  36.9 3.9 copy-start.27
  37.0 3.9 copy-start.28
  37.0 3.9 copy-start.29
  37.0 3.9 copy-start.30
  37.0 3.9 copy-start.31
  37.0 3.9 copy-start.32
  37.0 3.9 copy-start.33
  37.0 3.9 copy-start.34
  37.0 3.9 copy-start.35
  37.0 3.9 copy-start.36
  37.0 3.9 copy-start.37
  37.8 2.7 copy-start.1
  255.7 64.4 %copy-start.15 = (bf16[1,3,256,256]{3,2,1,0:T(8,128)(2,1)S(1)}, bf16[1,3,256,256]{3,2,1,0:T(8,128)(2,1)}, u32[]{:S(2)}) copy-start(bf16[1,3,256,256]{3,2,1,0:T(8,128)(2,1)} %param.25) | copy-start | bytes 1179652
  255.7 64.4 %copy-start.16 = (bf16[1,3,256,256]{3,2,1,0:T(8,128)(2,1)S(1)}, bf16[1,3,256,256]{3,2,1,0:T(8,128)(2,1)}, u32[]{:S(2)}) copy-start(bf16[1,3,256,256]{3,2,1,0:T(8,128)(2,1)} %param.26) | copy-start | bytes 1179652
  257.4 53.2 %collective-permute-start = (bf16[3,256,256]{2,1,0:T(8,128)(2,1)S(1)}, bf16[3,256,256]{2,1,0:T(8,128)(2,1)S(1)}, u32[]{:S(2)}, u32[]{:S(2)}) collective-permute-start(bf16[3,256,256]{2,1,0:T(8,128)(2,1)S(1)} %get-tuple-element.1576), channel_id=1, source_target_pairs={{8,0},{12,4},{16,8},{20,12},{24,16},{28,20},{32,24},{36,28},{40,32... | collective-permute-start | bytes 1179656 | tf_op jit(solution)/shard_map/ppermute | solution.py:14
  258.7 54.1 %collective-permute-start.1 = (bf16[3,256,256]{2,1,0:T(8,128)(2,1)S(1)}, bf16[3,256,256]{2,1,0:T(8,128)(2,1)S(1)}, u32[]{:S(2)}, u32[]{:S(2)}) collective-permute-start(bf16[3,256,256]{2,1,0:T(8,128)(2,1)S(1)} %get-tuple-element.1579), channel_id=1, source_target_pairs={{4,0},{8,4},{12,8},{16,12},{20,16},{24,20},{28,24},{32,28},{36,32}... | collective-permute-start | bytes 1179656 | tf_op jit(solution)/shard_map/ppermute | solution.py:14
  266.8 46.0 %collective-permute-start.2 = (bf16[3,256,256]{2,1,0:T(8,128)(2,1)S(1)}, bf16[3,256,256]{2,1,0:T(8,128)(2,1)S(1)}, u32[]{:S(2)}, u32[]{:S(2)}) collective-permute-start(bf16[3,256,256]{2,1,0:T(8,128)(2,1)S(1)} %get-tuple-element.1578), channel_id=1, source_target_pairs={{0,4},{4,8},{8,12},{12,16},{16,20},{20,24},{24,28},{28,32},{32,36}... | collective-permute-start | bytes 1179656 | tf_op jit(solution)/shard_map/ppermute | solution.py:14
  306.9 13.1 %collective-permute-start.3 = (bf16[3,256,256]{2,1,0:T(8,128)(2,1)S(1)}, bf16[3,256,256]{2,1,0:T(8,128)(2,1)S(1)}, u32[]{:S(2)}, u32[]{:S(2)}) collective-permute-start(bf16[3,256,256]{2,1,0:T(8,128)(2,1)S(1)} %get-tuple-element.1577), channel_id=1, source_target_pairs={{0,8},{4,12},{8,16},{12,20},{16,24},{20,28},{24,32},{28,36},{32,40... | collective-permute-start | bytes 1179656 | tf_op jit(solution)/shard_map/ppermute | solution.py:14
  320.4 12.7 %collective-permute-start.4 = (bf16[3,256,256]{2,1,0:T(8,128)(2,1)S(1)}, bf16[3,256,256]{2,1,0:T(8,128)(2,1)}, u32[]{:S(2)}, u32[]{:S(2)}) collective-permute-start(bf16[3,256,256]{2,1,0:T(8,128)(2,1)S(1)} %fusion.690), channel_id=1, source_target_pairs={{0,8},{4,12},{8,16},{12,20},{16,24},{20,28},{24,32},{28,36},{32,40... | collective-permute-start | bytes 1179656 | tf_op jit(solution)/shard_map/ppermute | solution.py:14
  325.0 12.3 %collective-permute-start.5 = (bf16[3,256,256]{2,1,0:T(8,128)(2,1)S(1)}, bf16[3,256,256]{2,1,0:T(8,128)(2,1)S(1)}, u32[]{:S(2)}, u32[]{:S(2)}) collective-permute-start(bf16[3,256,256]{2,1,0:T(8,128)(2,1)S(1)} %fusion.690), channel_id=1, source_target_pairs={{0,4},{4,8},{8,12},{12,16},{16,20},{20,24},{24,28},{28,32},{32,36}... | collective-permute-start | bytes 1179656 | tf_op jit(solution)/shard_map/ppermute | solution.py:14
  328.6 595.6 %all-reduce.4.cloned.1.call-start = ((), (), s32[]{:S(2)}) async-start(), calls=%async_computation.1 | async-start | bytes 4194304 | tf_op jit(solution)/shard_map/psum | solution.py:149
  328.6 42.3 %collective-permute-start.6 = (bf16[3,256,256]{2,1,0:T(8,128)(2,1)S(1)}, bf16[3,256,256]{2,1,0:T(8,128)(2,1)S(1)}, u32[]{:S(2)}, u32[]{:S(2)}) collective-permute-start(bf16[3,256,256]{2,1,0:T(8,128)(2,1)S(1)} %fusion.690), channel_id=1, source_target_pairs={{4,0},{8,4},{12,8},{16,12},{20,16},{24,20},{28,24},{32,28},{36,32}... | collective-permute-start | bytes 1179656 | tf_op jit(solution)/shard_map/ppermute | solution.py:14
  330.6 48.8 %collective-permute-start.7 = (bf16[3,256,256]{2,1,0:T(8,128)(2,1)S(1)}, bf16[3,256,256]{2,1,0:T(8,128)(2,1)S(1)}, u32[]{:S(2)}, u32[]{:S(2)}) collective-permute-start(bf16[3,256,256]{2,1,0:T(8,128)(2,1)S(1)} %fusion.690), channel_id=1, source_target_pairs={{8,0},{12,4},{16,8},{20,12},{24,16},{28,20},{32,24},{36,28},{40,32... | collective-permute-start | bytes 1179656 | tf_op jit(solution)/shard_map/ppermute | solution.py:14
  (2 other events, 3.7 us)
Sparse Core Ops, SparseCore 0:
  328.7 159.8 all-gather.1
  592.4 331.7 all-reduce.3
where the time goes:
time: 944 us; the launch traced here: 935 us
  waiting for transfers between devices  388 us (41%)
  loops' own time  247 us (26%)
  matrix products  89.9 us (10%)
  other arithmetic  67.3 us (7%)
  local copies, waits for them, and re-layouts  64.1 us (7%)
  starting transfers between devices  63.6 us (7%)
  between operations  14.9 us (2%)
    psum x1, waiting for transfers between devices, body(): summed = lax.psum((sample_grad, sample_grad * scale_map * eps_float), 'mc')  332 us
    another operation x3, loops' own time, body(): lax.fori_loop(0, my_counts[filt_id], place_slot, empty_rows)  124 us
    another operation x3, loops' own time, body(): grad_rows.append(lax.fori_loop(0, my_counts[filt_id], add_back, zero_image))  123 us
    ppermute x8, starting transfers between devices, shifted(): return lax.ppermute(x, axis, pairs)  63.5 us
    ppermute x8, waiting for transfers between devices, shifted(): return lax.ppermute(x, axis, pairs)  55.9 us
    dot_general x30, matrix products, adjoint_term(): jnp.dot(back_half, cols_matrix, preferred_element_type=jnp.float32)  42.6 us
    dot_general x30, matrix products, contribution(): lax.dot_general(half_blur, cols_matrix, (((1,), (1,)), ((), ())), preferr...  40.3 us
    add x60, other arithmetic, weight_map(): coeff_f[0] + coeff_f[1] * centred[:, None] + coeff_f[2] * centred[None, :]  38.7 us
  transfers between devices with their start and end apart: 10, of which 8 were waited for; matrix products, arithmetic and copies ran while one was open for 9% of the time, Pallas kernels for 0%

commit v1 on v0

v1 whole, which is shorter than its diff:
```python
import functools

import jax
import jax.numpy as jnp
from jax import lax
from jax.experimental import pallas as pl
from jax.experimental.pallas import tpu as pltpu
from jax.sharding import PartitionSpec as P

NB = 6
K = 3
REACH = 2
WINDOW = 2 * REACH + 1
MESH = pl.DeviceIdType.MESH
F32 = jnp.float32
BF16 = jnp.bfloat16


def dot(a, b):
    return jnp.dot(a, b, preferred_element_type=F32)


def band_rows(pat, a, side):
    half = side // 2
    start = (16 * a - 12) % half
    rolled = pltpu.roll(pat, start, 1) if start else pat
    lane = lax.broadcasted_iota(jnp.int32, rolled.shape, 1)
    zero = jnp.zeros_like(rolled)
    low = jnp.where(lane < half // 2, rolled, zero)
    high = jnp.where(lane >= half // 2, rolled, zero)
    blocks = half // 16
    if a == 0:
        return low, zero
    if a < blocks - 1:
        return rolled, zero
    if a <= blocks:
        return high, low
    if a < 2 * blocks - 1:
        return zero, rolled
    return zero, high


def kernel(
    tiles,
    taps_ref,
    itab,
    ftab,
    mean_hbm,
    lsc_hbm,
    noise_hbm,
    obs_hbm,
    ivar_hbm,
    mu_hbm,
    rho_hbm,
    mean,
    scale,
    noise,
    obs,
    ivar,
    diff,
    lrow,
    rmat,
    rmat_t,
    cmat,
    cmat_t,
    x_ref,
    blur,
    mixed,
    placed,
    own,
    send_p,
    recv_p,
    send_d,
    recv_d,
    send_q,
    recv_q,
    near0,
    near1,
    near2,
    moved,
    half,
    send_g,
    recv_g,
    e_ref,
    pri_mu,
    pri_rho,
    mu,
    rho,
    in_sem,
    out_sem,
    noise_sem,
    p_sem,
    d_sem,
    q_sem,
    rp_sem,
    ru_sem,
    rd_sem,
    relay_sem,
    g_sem,
    e_sem,
):
    filters, side = mean.shape[0], mean.shape[1]
    nbasis = rmat.shape[0]
    near = (near0, near1, near2)
    t = lax.axis_index("tile")
    s = lax.axis_index("mc")
    h = lax.axis_index("filt")
    sigma = 1 - 2 * lax.rem(t, 2)
    partner = {"tile": t + sigma}
    ahead = {"tile": lax.rem(t + 2 * sigma + tiles, tiles)}
    behind = {"tile": lax.rem(t - 2 * sigma + tiles, tiles)}
    twin = {"mc": 1 - s}
    across = {"filt": 1 - h, "mc": 1 - s}

    i_k, i_oy, i_ox, i_e, i_sel = 0, 54, 63, 72, 81
    f_c, f_a, f_p = 0, 162, 378

    def remote(src, dst, sem, f, to):
        return pltpu.make_async_remote_copy(
            src_ref=src,
            dst_ref=dst,
            send_sem=sem.at[0, f],
            recv_sem=sem.at[1, f],
            device_id=to,
            device_id_type=MESH,
        )

    loads = []
    for f in range(filters):
        loads.append(
            [
                pltpu.make_async_copy(noise_hbm.at[f], noise.at[s, f], in_sem.at[0, f]),
                pltpu.make_async_copy(mean_hbm.at[f], mean.at[f], in_sem.at[1, f]),
                pltpu.make_async_copy(lsc_hbm.at[f], scale.at[f], in_sem.at[2, f]),
            ]
        )
    late = [
        pltpu.make_async_copy(obs_hbm, obs, in_sem.at[3, 0]),
        pltpu.make_async_copy(ivar_hbm, ivar, in_sem.at[3, 1]),
    ]
    for group in loads:
        for copy in group:
            copy.start()
    for copy in late:
        copy.start()

    barrier = pltpu.get_barrier_semaphore()
    for to in (partner, ahead, behind, twin, across):
        pl.semaphore_signal(barrier, inc=1, device_id=to, device_id_type=MESH)

    rows_i = lax.broadcasted_iota(jnp.int32, (side, side), 0)
    cols_i = lax.broadcasted_iota(jnp.int32, (side, side), 1)
    diff[...] = rows_i - cols_i
    centre_i = lax.broadcasted_iota(jnp.int32, (side, 128), 0)
    lrow[...] = (2 * centre_i + 1 - side).astype(F32) * (1.0 / side)
    centre_j = lax.broadcasted_iota(jnp.int32, (1, side), 1)
    lcol = (2 * centre_j + 1 - side).astype(F32) * (1.0 / side)
    placed[K] = jnp.zeros((side, side), BF16)

    def build(dst, first, stride):
        def one(k, carry):
            row = taps_ref[pl.ds(first + stride * k, 1), :]
            pat = jnp.broadcast_to(row, (16, 128))
            pat = pltpu.roll(pat, 0, 1, stride=1, stride_axis=0)
            for a in range(side // 16):
                left, right = band_rows(pat, a, side)
                dst[k, 16 * a : 16 * a + 16, 0:128] = left.astype(BF16)
                dst[k, 16 * a : 16 * a + 16, 128:256] = right.astype(BF16)
            return carry

        lax.fori_loop(0, nbasis, one, 0)

    def build_flat(dst, first, stride):
        def one(k, carry):
            row = taps_ref[pl.ds(first + stride * k, 1), :]
            pat = jnp.broadcast_to(row, (16, 128))
            pat = pltpu.roll(pat, 0, 1, stride=1, stride_axis=0)
            for a in range(side // 16):
                left, right = band_rows(pat, a, side)
                at = pl.ds(pl.multiple_of(k * side + 16 * a, 16), 16)
                dst[at, 0:128] = left.astype(BF16)
                dst[at, 128:256] = right.astype(BF16)
            return carry

        lax.fori_loop(0, nbasis, one, 0)

    build(rmat, 2 * nbasis, 2)
    build(cmat_t, 1, 2)

    for f in range(filters):
        loads[f][0].wait()
    pl.semaphore_wait(barrier, 5)
    noise_out = remote(noise.at[s], noise.at[s], noise_sem, 0, twin)
    noise_out.start()

    chunk = 32
    chunks = side // chunk

    def over_rows(body):
        def one(r, carry):
            body(pl.ds(pl.multiple_of(r * chunk, chunk), chunk))
            return carry

        lax.fori_loop(0, chunks, one, 0)

    def shift_matrix(offset):
        return jnp.where(diff[...] == offset, 1.0, 0.0).astype(BF16)

    def forward(f):
        def sample_rows(rows):
            sc = jnp.exp(scale[f, rows, :])
            scale[f, rows, :] = sc
            x_ref[rows, :] = (mean[f, rows, :] + sc * noise[s, f, rows, :].astype(F32)).astype(BF16)

        over_rows(sample_rows)

        def blur_one(k, carry):
            hb = dot(rmat[k], x_ref[...]).astype(BF16)
            blur[k] = dot(hb, cmat_t[k])
            return carry

        lax.fori_loop(0, nbasis, blur_one, 0, unroll=2)

        def slot(q, carry):
            fq = f * K + q
            base = f_c + fq * NB * 3
            c0 = [ftab[base + 3 * b] for b in range(NB)]
            c1 = [ftab[base + 3 * b + 1] for b in range(NB)]
            c2 = [ftab[base + 3 * b + 2] for b in range(NB)]
            kb = [itab[i_k + fq * NB + b] for b in range(NB)]
            beta = [c2[b] * lcol for b in range(NB)]

            def mix_rows(rows):
                li = lrow[rows, :]
                alpha = [c0[b] + c1[b] * li for b in range(NB)]
                for lo in (0, 128):
                    acc = None
                    for b in range(NB):
                        term = (alpha[b] + beta[b][:, lo : lo + 128]) * blur[kb[b], rows, lo : lo + 128]
                        acc = term if acc is None else acc + term
                    mixed[rows, lo : lo + 128] = acc.astype(BF16)

            over_rows(mix_rows)
            oy = itab[i_oy + fq]
            ox = itab[i_ox + fq]
            part = dot(shift_matrix(oy), mixed[...]).astype(BF16)
            placed[q] = dot(part, shift_matrix(-ox)).astype(BF16)
            return carry

        lax.fori_loop(0, K, slot, 0)

        def pick(d):
            return placed[itab[i_sel + f * WINDOW + d]]

        own[f] = pick(REACH)
        send_p[f, 0] = pick(REACH + sigma)
        send_p[f, 1] = pick(REACH - sigma)
        send_d[f] = pick(REACH - 2 * sigma)
        send_q[f] = pick(REACH + 2 * sigma)

    def p_copy(f):
        return remote(send_p.at[f], recv_p.at[f], p_sem, f, partner)

    def d_copy(f):
        return remote(send_d.at[f], recv_d.at[f], d_sem, f, behind)

    def q_copy(f):
        return remote(send_q.at[f], recv_q.at[f], q_sem, f, ahead)

    def merge(f):
        p_copy(f).wait_recv()

        def rows_of(rows):
            joined = send_q[f, rows, :].astype(F32) + recv_p[f, 1, rows, :].astype(F32)
            send_q[f, rows, :] = joined.astype(BF16)

        over_rows(rows_of)
        q_copy(f).start()

    for f in range(filters):
        loads[f][1].wait()
        loads[f][2].wait()
        forward(f)
        p_copy(f).start()
        d_copy(f).start()
        if f > 0:
            merge(f - 1)
    merge(filters - 1)

    noise_out.wait_recv()

    def g_copy(f):
        return remote(send_g.at[f], recv_g.at[f], g_sem, f, across)

    for f in range(filters):

        def twin_rows(rows):
            other = noise[1 - s, f, rows, :].astype(F32)
            send_g[f, rows, :] = (mean[f, rows, :] + scale[f, rows, :] * other).astype(BF16)

        over_rows(twin_rows)
        g_copy(f).start()

    build(rmat_t, 0, 2)
    build_flat(cmat, 2 * nbasis + 1, 2)

    def rp_copy(f):
        return remote(near[f].at[REACH], near[f].at[REACH - sigma], rp_sem, f, partner)

    def ru_copy(f):
        return remote(near[f].at[REACH], near[f].at[REACH - 2 * sigma], ru_sem, f, ahead)

    def rd_copy(f):
        return remote(near[f].at[REACH], near[f].at[REACH + 2 * sigma], rd_sem, f, behind)

    def relay_copy(f):
        return remote(near[f].at[REACH + 2 * sigma], near[f].at[REACH + sigma], relay_sem, f, partner)

    for copy in late:
        copy.wait()

    def residual(f):
        d_copy(f).wait_recv()
        q_copy(f).wait_recv()

        def rows_of(rows):
            pred = own[f, rows, :].astype(F32) + recv_p[f, 0, rows, :].astype(F32)
            pred = pred + recv_d[f, rows, :].astype(F32) + recv_q[f, rows, :].astype(F32)
            res = ivar[f, rows, :].astype(F32) * (obs[f, rows, :].astype(F32) - pred)
            near[f][REACH, rows, :] = res.astype(BF16)

        over_rows(rows_of)
        ru_copy(f).start()
        rd_copy(f).start()
        rp_copy(f).start()

    def own_prior(f):
        prec = [ftab[f_p + f * 6 + g] for g in range(filters)]

        def rows_of(rows):
            sc = scale[f, rows, :]
            pri, dev = [], []
            for which in range(2):
                total = None
                for g in range(filters):
                    sam = mean[g, rows, :] + scale[g, rows, :] * noise[which, g, rows, :].astype(F32)
                    total = prec[g] * sam if total is None else total + prec[g] * sam
                pri.append(total)
                dev.append(sc * noise[which, f, rows, :].astype(F32))
            pri_mu[f, rows, :] = 0.5 * (pri[0] + pri[1])
            pri_rho[f, rows, :] = 1.0 - 0.5 * (pri[0] * dev[0] + pri[1] * dev[1])

        over_rows(rows_of)

    def backward(f):
        ru_copy(f).wait_recv()
        rp_copy(f).wait_recv()
        relay_copy(f).wait_recv()

        def pull(q, carry):
            fq = f * K + q
            oy = itab[i_oy + fq]
            ox = itab[i_ox + fq]
            part = dot(shift_matrix(-oy), near[f][itab[i_e + fq]]).astype(BF16)
            moved[q] = dot(part, shift_matrix(ox))
            return carry

        lax.fori_loop(0, K, pull, 0)

        def adjoint(k, carry):
            coef = [
                [ftab[f_a + ((f * K + q) * nbasis + k) * 3 + m] for m in range(3)] for q in range(K)
            ]
            beta = [coef[q][2] * lcol for q in range(K)]

            def weigh_rows(rows):
                li = lrow[rows, :]
                alpha = [coef[q][0] + coef[q][1] * li for q in range(K)]
                for lo in (0, 128):
                    acc = None
                    for q in range(K):
                        term = (alpha[q] + beta[q][:, lo : lo + 128]) * moved[q, rows, lo : lo + 128]
                        acc = term if acc is None else acc + term
                    x_ref[rows, lo : lo + 128] = acc.astype(BF16)

            over_rows(weigh_rows)
            at = pl.ds(pl.multiple_of(k * side, side), side)
            half[:, at] = dot(rmat_t[k], x_ref[...]).astype(BF16)
            return carry

        lax.fori_loop(0, nbasis, adjoint, 0)
        prec = [ftab[f_p + f * 6 + filters + g] for g in range(filters)]

        def finish_rows(rows):
            grad = dot(half[rows, :], cmat[...])
            for g in range(filters):
                grad = grad - prec[g] * recv_g[g, rows, :].astype(F32)
            e_ref[s, f, rows, :] = grad.astype(BF16)

        def finish(r, carry):
            finish_rows(pl.ds(pl.multiple_of(r * 128, 128), 128))
            return carry

        lax.fori_loop(0, side // 128, finish, 0)
        e_copy(f).start()

    def e_copy(f):
        return remote(e_ref.at[s, f], e_ref.at[s, f], e_sem, f, twin)

    def outs(f):
        return (
            pltpu.make_async_copy(mu.at[f], mu_hbm.at[f], out_sem.at[0, f]),
            pltpu.make_async_copy(rho.at[f], rho_hbm.at[f], out_sem.at[1, f]),
        )

    def final(f):
        e_copy(f).wait_recv()

        def rows_of(rows):
            sc = scale[f, rows, :]
            e0 = e_ref[0, f, rows, :].astype(F32)
            e1 = e_ref[1, f, rows, :].astype(F32)
            d0 = sc * noise[0, f, rows, :].astype(F32)
            d1 = sc * noise[1, f, rows, :].astype(F32)
            mu[f, rows, :] = 0.5 * (e0 + e1) - pri_mu[f, rows, :]
            rho[f, rows, :] = 0.5 * (e0 * d0 + e1 * d1) + pri_rho[f, rows, :]

        over_rows(rows_of)
        for copy in outs(f):
            copy.start()

    def relay(f):
        rd_copy(f).wait_recv()
        relay_copy(f).start()

    for f in range(filters):
        residual(f)
    relay(0)
    for f in range(filters):
        own_prior(f)
    for f in range(filters):
        g_copy(f).wait_recv()
    backward(0)
    relay(1)
    backward(1)
    final(0)
    relay(2)
    backward(2)
    final(1)
    final(2)

    noise_out.wait_send()
    for f in range(filters):
        for copy in (p_copy, d_copy, q_copy, g_copy, ru_copy, rd_copy, rp_copy, relay_copy, e_copy):
            copy(f).wait_send()
        for copy in outs(f):
            copy.wait()


def tables(intersections, counts, psf_coeffs, prior_prec, nbasis, local_filters):
    tile_here = lax.axis_index("tile")
    first = lax.axis_index("filt") * local_filters
    fields = intersections.shape[3]
    exposures = psf_coeffs.shape[0]
    side_scale = 1.0 / 128.0
    slots = lax.dynamic_slice(intersections, (tile_here, first, 0, 0), (1, local_filters, K, fields))[0]
    live_count = lax.dynamic_slice(counts, (tile_here, first), (1, local_filters))[0]
    start = jnp.clip(tile_here - REACH, 0, exposures - WINDOW)
    psf = lax.dynamic_slice(psf_coeffs, (start, first, 0, 0), (WINDOW, local_filters, NB, 3)).astype(F32)
    live = jnp.arange(K)[None, :] < live_count[:, None]
    exposure, oy, ox, kb = slots[..., 0], slots[..., 1], slots[..., 2], slots[..., 3:]
    which = jnp.where(live, exposure - start, -1)
    hit = (which[:, :, None] == jnp.arange(WINDOW)[None, None, :]).astype(F32)
    coef = jnp.sum(hit[:, :, :, None, None] * jnp.transpose(psf, (1, 0, 2, 3))[:, None], axis=2)
    shift_y = oy.astype(F32)[:, :, None] * side_scale
    shift_x = ox.astype(F32)[:, :, None] * side_scale
    c0 = coef[..., 0] + coef[..., 1] * shift_y + coef[..., 2] * shift_x
    coef = jnp.stack([c0, coef[..., 1], coef[..., 2]], -1)
    onehot = (kb[..., None] == jnp.arange(nbasis)).astype(F32)
    per_basis = jnp.sum(onehot[..., None] * coef[:, :, :, None, :], axis=2)
    place = exposure - tile_here + REACH
    wanted = live[:, :, None] & (place[:, :, None] == jnp.arange(WINDOW))
    select = jnp.min(jnp.where(wanted, jnp.arange(K)[None, :, None], K), axis=1)
    prec = lax.dynamic_slice(prior_prec, (first, 0), (local_filters, prior_prec.shape[1]))
    rolled = jnp.where(first > 0, jnp.concatenate([prec[:, local_filters:], prec[:, :local_filters]], 1), prec)
    ints = [kb, oy, ox, jnp.clip(place, 0, WINDOW - 1), select]
    floats = [coef, per_basis, rolled]
    itab = jnp.concatenate([v.reshape(-1) for v in ints]).astype(jnp.int32)
    ftab = jnp.concatenate([v.reshape(-1) for v in floats])
    return itab, ftab


def body(tiles, sky_mean, sky_log_scale, noise_draw, observed, inv_var, intersections, counts, kernels, psf_coeffs, prior_prec):
    filters, side = sky_mean.shape[1], sky_mean.shape[2]
    nbasis, _, taps = kernels.shape
    itab, ftab = tables(intersections, counts, psf_coeffs, prior_prec, nbasis, filters)
    flat = kernels.reshape(2 * nbasis, taps)
    tap_rows = jnp.pad(jnp.concatenate([flat, flat[:, ::-1]], 0), ((0, 0), (0, 128 - taps)))
    img = (side, side)
    anyspec = pl.BlockSpec(memory_space=pl.ANY)
    vmem = pltpu.VMEM
    dma = pltpu.SemaphoreType.DMA
    mu, rho = pl.pallas_call(
        functools.partial(kernel, tiles),
        out_shape=[jax.ShapeDtypeStruct((filters,) + img, F32)] * 2,
        in_specs=[
            pl.BlockSpec(memory_space=pltpu.VMEM),
            pl.BlockSpec(memory_space=pltpu.SMEM),
            pl.BlockSpec(memory_space=pltpu.SMEM),
        ]
        + [anyspec] * 5,
        out_specs=[anyspec] * 2,
        scratch_shapes=[
            vmem((filters,) + img, F32),
            vmem((filters,) + img, F32),
            vmem((2, filters) + img, BF16),
            vmem((filters,) + img, BF16),
            vmem((filters,) + img, BF16),
            vmem(img, jnp.int32),
            vmem((side, 128), F32),
            vmem((nbasis,) + img, BF16),
            vmem((nbasis,) + img, BF16),
            vmem((nbasis * side, side), BF16),
            vmem((nbasis,) + img, BF16),
            vmem(img, BF16),
            vmem((nbasis,) + img, F32),
            vmem(img, BF16),
            vmem((K + 1,) + img, BF16),
            vmem((filters,) + img, BF16),
            vmem((filters, 2) + img, BF16),
            vmem((filters, 2) + img, BF16),
            vmem((filters,) + img, BF16),
            vmem((filters,) + img, BF16),
            vmem((filters,) + img, BF16),
            vmem((filters,) + img, BF16),
            vmem((WINDOW,) + img, BF16),
            vmem((WINDOW,) + img, BF16),
            vmem((WINDOW,) + img, BF16),
            vmem((K,) + img, F32),
            vmem((side, nbasis * side), BF16),
            vmem((filters,) + img, BF16),
            vmem((filters,) + img, BF16),
            vmem((2, filters) + img, BF16),
            vmem((filters,) + img, F32),
            vmem((filters,) + img, F32),
            vmem((filters,) + img, F32),
            vmem((filters,) + img, F32),
            dma((4, filters)),
            dma((2, filters)),
            dma((2, 1)),
        ]
        + [dma((2, filters))] * 9,
        compiler_params=pltpu.CompilerParams(
            collective_id=0, has_side_effects=True, vmem_limit_bytes=48 * 1024 * 1024
        ),
    )(tap_rows, itab, ftab, sky_mean[0], sky_log_scale[0], noise_draw[0, 0], observed[0], inv_var[0])
    return mu[None], rho[None]


def solution(mesh):
    placed = (
        P("tile", "filt", None, None),
        P("tile", "filt", None, None),
        P("mc", "tile", "filt", None, None),
        P("tile", "filt", None, None),
        P("tile", "filt", None, None),
        P(),
        P(),
        P(),
        P(),
        P(),
    )
    return jax.shard_map(
        functools.partial(body, mesh.shape["tile"]),
        mesh=mesh,
        in_specs=placed,
        out_specs=(P("tile", "filt", None, None), P("tile", "filt", None, None)),
        check_vma=False,
    )
```

time: 944 us -> 75.2 us (0.08)
  waiting for transfers between devices: 388 us -> 0 us
  loops' own time: 247 us -> 0 us
  matrix products: 89.9 us -> 0 us
  other arithmetic: 67.3 us -> 3.62 us
  starting transfers between devices: 63.6 us -> 0 us
  Pallas kernels: 0 us -> 60.4 us
  local copies, waits for them, and re-layouts: 64.1 us -> 10 us
  between operations: 14.9 us -> 0.74 us
    psum x1 -> x0, waiting for transfers between devices: 332 us -> none  [body(): summed = lax.psum((sample_grad, sample_grad * scale_map * eps_float), 'mc')]
    another operation x6 -> x0, loops' own time: 247 us -> none  [the longest x3 124 us: body(): lax.fori_loop(0, my_counts[filt_id], place_slot, empty_rows)]
    dot_general x61 -> x0, matrix products: 89.9 us -> none  [the longest x30 42.6 us: adjoint_term(): jnp.dot(back_half, cols_matrix, preferred_element_type=jnp.float32)]
    ppermute x8 -> x0, starting transfers between devices: 63.5 us -> none  [shifted(): return lax.ppermute(x, axis, pairs)]
    pallas_call x0 -> x1, Pallas kernels: none -> 60.4 us  [body(): pl.pallas_call(functools.partial(kernel, tiles), out_shape=[jax.ShapeDtyp...]
    ppermute x8 -> x0, waiting for transfers between devices: 55.9 us -> none  [shifted(): return lax.ppermute(x, axis, pairs)]
    add x60 -> x1, other arithmetic: 38.7 us -> 0.09 us  [tables(): c0 = coef[..., 0] + coef[..., 1] * shift_y + coef[..., 2] * shift_x]
    slice x68 -> x3, local copies, waits for them, and re-layouts: 30.4 us -> 0.15 us  [the longest x1 0.07 us: tables(): prec[:, local_filters:]]
  transfers between devices with their start and end apart: 10 -> 0, of which waited for: 8 -> 0; matrix products, arithmetic and copies ran while one was open for 9% -> 0% of each run, Pallas kernels for 0% -> 0%
where the time goes in v1:
time: 75.2 us; the launch traced here: 74.7 us
  Pallas kernels  60.4 us (80%)
  local copies, waits for them, and re-layouts  10 us (13%)
  other arithmetic  3.62 us (5%)
    pallas_call x1, Pallas kernels, body(): pl.pallas_call(functools.partial(kernel, tiles), out_shape=[jax.ShapeDtyp...  60.4 us
    unnamed x14, local copies, waits for them, and re-layouts  5.9 us

profile of v1, /device:TPU:1, one launch (start us, length us, event | category | flops | bytes accessed | tf_op | source)
XLA Modules:
  0.0 74.7 jit_solution(13914915267534834190)
XLA Ops:
  0.6 0.0 copy-start
  0.6 0.0 copy-start.1
  0.7 1.0 %dynamic-slice_reduce_fusion = s32[3]{0:T(128)S(1)} fusion(s32[128,6]{0,1:T(8,128)} %param.16, s32[]{:T(128)S(6)} %select_n.28, s32[]{:T(128)S(6)} %select_n.29), kind=kLoop, calls=%fused_computation.28 | loop fusion | bytes 32 | tf_op jit(solution)/shard_map/dynamic_slice | solution.py:467
  1.6 0.1 iota_compare_fusion.5
  1.7 0.7 constant_dynamic-slice_fusion
  2.4 0.1 fusion.6
  2.5 0.8 %maximum_select_fusion = f32[3,6]{1,0:T(4,128)S(1)} fusion(f32[3,3]{1,0:T(4,128)S(1)} %get-tuple-element.14, f32[3,3]{1,0:T(4,128)S(1)} %get-tuple-element.13, pred[]{:T(512)S(6)} %gt.3, f32[6,6]{1,0:T(8,128)} %param.19, s32[]{:T(128)S(6)} %select_n.29), kind=kLoop, calls=%fused_computation.26 | loop fusion | flops 36 | bytes 221 | tf_op jit(solution)/shard_map/jit(_where)/select_n | solution.py:485
  3.2 0.1 reshape.99
  3.3 0.8 %rev.3 = f32[16,25]{1,0:T(8,128)S(1)} reverse(f32[16,25]{1,0:T(8,128)} %bitcast.23), dimensions={1} | reverse | bytes 3200 | tf_op jit(solution)/shard_map/rev | solution.py:498
  4.1 0.7 select_maximum_fusion.taps_ref
  4.8 0.8 %convert_bitcast_fusion = f32[3,5,6,3]{1,3,2,0:T(4,128)S(1)} fusion(bf16[128,6,6,3]{0,3,2,1:T(4,128)(2,1)} %param.18, s32[]{:T(128)S(6)} %min.17, s32[]{:T(128)S(6)} %select_n.29), kind=kLoop, calls=%fused_computation.2 | loop fusion | flops 270 | bytes 1628 | tf_op jit(solution)/shard_map/transpose | solution.py:474
  5.6 0.2 copy.17
  5.8 0.0 copy-done
  5.8 0.1 constant_dynamic-slice_fusion.1
  5.9 0.2 copy.16
  6.0 0.2 multiply_reduce_fusion.3
  6.2 0.1 slice.42
  6.2 0.1 reshape.95
  6.3 0.4 select_reduce_fusion
  6.8 0.1 min.16
  6.9 0.1 reshape_squeeze.7
  6.9 0.1 reshape_squeeze.6
  7.0 0.1 select_reduce_fusion.1
  7.1 0.1 reshape.96
  7.2 0.1 concatenate.13.itab
  7.3 0.1 fusion.2
  7.4 0.1 multiply_reduce_fusion.1
  7.5 0.1 fusion.3
  7.6 0.1 fusion
  7.7 0.1 multiply_reduce_fusion
  7.8 0.1 copy.18
  8.0 0.1 reshape.97
  8.1 0.1 copy.19
  8.2 0.1 reshape.98
  8.4 0.1 pad_maximum_fusion.1.ftab
  8.5 0.0 copy-done.1
  8.5 0.0 copy-start.2
  8.5 1.1 %copy-done.2 = f32[1,3,256,256]{3,2,1,0:T(8,128)S(1)} copy-done((f32[1,3,256,256]{3,2,1,0:T(8,128)S(1)}, f32[1,3,256,256]{3,2,1,0:T(8,128)}, u32[]{:S(2)}) %copy-start.2) | copy-done | bytes 786456
  9.6 0.0 copy-start.3
  9.6 1.0 %copy-done.3 = bf16[1,1,3,256,256]{4,3,2,1,0:T(8,128)(2,1)S(1)} copy-done((bf16[1,1,3,256,256]{4,3,2,1,0:T(8,128)(2,1)S(1)}, bf16[1,1,3,256,256]{4,3,2,1,0:T(8,128)(2,1)}, u32[]{:S(2)}) %copy-start.3) | copy-done | bytes 393240
  10.6 0.0 copy-start.4
  10.6 1.0 %copy-done.4 = bf16[1,3,256,256]{3,2,1,0:T(8,128)(2,1)S(1)} copy-done((bf16[1,3,256,256]{3,2,1,0:T(8,128)(2,1)S(1)}, bf16[1,3,256,256]{3,2,1,0:T(8,128)(2,1)}, u32[]{:S(2)}) %copy-start.4) | copy-done | bytes 393240
  11.6 0.0 copy-start.5
  11.6 1.0 %copy-done.5 = bf16[1,3,256,256]{3,2,1,0:T(8,128)(2,1)S(1)} copy-done((bf16[1,3,256,256]{3,2,1,0:T(8,128)(2,1)S(1)}, bf16[1,3,256,256]{3,2,1,0:T(8,128)(2,1)}, u32[]{:S(2)}) %copy-start.5) | copy-done | bytes 393240
  12.6 60.4 %shard_map.113 = (f32[3,256,256]{2,1,0:T(8,128)S(1)}, f32[3,256,256]{2,1,0:T(8,128)S(1)}) custom-call(f32[32,128]{1,0:T(8,128)S(1)} %select_maximum_fusion.taps_ref, s32[96]{0:T(128)S(1)} %concatenate.13.itab, f32[396]{0:T(512)S(1)} %pad_maximum_fusion.1.ftab, f32[3,256,256]{2,1,0:T(8,128)S(1)} %bitcast.15, f32[3,256,256]{2,1,0:T(8,128)S(1)} %bitcast.16, ...), custom_call_target="tpu_custom_call" | custom-call | tf_op jit(solution)/shard_map/pallas_call | solution.py:503
  73.0 0.9 %copy.22 = f32[1,3,256,256]{3,2,1,0:T(8,128)} copy(f32[1,3,256,256]{3,2,1,0:T(8,128)S(1)} %bitcast.14) | data formatting | bytes 1572864
  73.9 0.9 %copy.23 = f32[1,3,256,256]{3,2,1,0:T(8,128)} copy(f32[1,3,256,256]{3,2,1,0:T(8,128)S(1)} %bitcast.13) | data formatting | bytes 1572864
  (2 shorter events, 0.0 us)
Async XLA Ops:
  0.6 5.1 %copy-start = (s32[128,6,3,9]{0,2,3,1:T(4,128)S(1)}, s32[128,6,3,9]{0,2,3,1:T(4,128)}, u32[]{:S(2)}) copy-start(s32[128,6,3,9]{0,2,3,1:T(4,128)} %param.15) | copy-start | bytes 248836
  0.6 7.8 %copy-start.1 = (f32[1,3,256,256]{3,2,1,0:T(8,128)S(1)}, f32[1,3,256,256]{3,2,1,0:T(8,128)}, u32[]{:S(2)}) copy-start(f32[1,3,256,256]{3,2,1,0:T(8,128)} %param.10) | copy-start | bytes 2359300
  8.5 1.1 %copy-start.2 = (f32[1,3,256,256]{3,2,1,0:T(8,128)S(1)}, f32[1,3,256,256]{3,2,1,0:T(8,128)}, u32[]{:S(2)}) copy-start(f32[1,3,256,256]{3,2,1,0:T(8,128)} %param.11) | copy-start | bytes 2359300
  9.6 1.0 %copy-start.3 = (bf16[1,1,3,256,256]{4,3,2,1,0:T(8,128)(2,1)S(1)}, bf16[1,1,3,256,256]{4,3,2,1,0:T(8,128)(2,1)}, u32[]{:S(2)}) copy-start(bf16[1,1,3,256,256]{4,3,2,1,0:T(8,128)(2,1)} %param.12) | copy-start | bytes 1179652
  10.6 1.0 %copy-start.4 = (bf16[1,3,256,256]{3,2,1,0:T(8,128)(2,1)S(1)}, bf16[1,3,256,256]{3,2,1,0:T(8,128)(2,1)}, u32[]{:S(2)}) copy-start(bf16[1,3,256,256]{3,2,1,0:T(8,128)(2,1)} %param.13) | copy-start | bytes 1179652
  11.6 1.0 %copy-start.5 = (bf16[1,3,256,256]{3,2,1,0:T(8,128)(2,1)S(1)}, bf16[1,3,256,256]{3,2,1,0:T(8,128)(2,1)}, u32[]{:S(2)}) copy-start(bf16[1,3,256,256]{3,2,1,0:T(8,128)(2,1)} %param.14) | copy-start | bytes 1179652

commit v2 on v1

v2 whole, which is shorter than its diff:
```python
import functools

import jax
import jax.numpy as jnp
from jax import lax
from jax.experimental import pallas as pl
from jax.experimental.pallas import tpu as pltpu
from jax.sharding import PartitionSpec as P

NB = 6
K = 3
STRIP = 16
REACH = 2
WINDOW = 2 * REACH + 1
MESH = pl.DeviceIdType.MESH
F32 = jnp.float32
BF16 = jnp.bfloat16


def dot(a, b):
    return jnp.dot(a, b, preferred_element_type=F32)


def band_rows(pat, a, side):
    half = side // 2
    start = (16 * a - 12) % half
    rolled = pltpu.roll(pat, start, 1) if start else pat
    lane = lax.broadcasted_iota(jnp.int32, rolled.shape, 1)
    zero = jnp.zeros_like(rolled)
    low = jnp.where(lane < half // 2, rolled, zero)
    high = jnp.where(lane >= half // 2, rolled, zero)
    blocks = half // 16
    if a == 0:
        return low, zero
    if a < blocks - 1:
        return rolled, zero
    if a <= blocks:
        return high, low
    if a < 2 * blocks - 1:
        return zero, rolled
    return zero, high


def kernel(
    tiles,
    kern_hbm,
    inter_hbm,
    count_hbm,
    psf_hbm,
    prec_hbm,
    mean_hbm,
    lsc_hbm,
    noise_hbm,
    obs_hbm,
    ivar_hbm,
    mu,
    rho,
    kern,
    taps,
    inter,
    count,
    psf_b,
    psf_f,
    psf,
    prec,
    basis_v,
    per_basis,
    mean,
    scale,
    noise,
    obs,
    ivar,
    lrow,
    rmat,
    rmat_t,
    cmat,
    cmat_t,
    x_ref,
    y_ref,
    half_blur,
    blur,
    turn,
    placed,
    own,
    send_p,
    recv_p,
    send_d,
    recv_d,
    send_q,
    recv_q,
    near0,
    near1,
    near2,
    moved,
    half,
    send_g,
    recv_g,
    e_ref,
    pri_mu,
    pri_rho,
    in_sem,
    tab_sem,
    noise_sem,
    p_sem,
    d_sem,
    q_sem,
    rp_sem,
    ru_sem,
    rd_sem,
    relay_sem,
    g_sem,
    e_sem,
):
    filters, side = mean.shape[0], mean.shape[1]
    nbasis = rmat_t.shape[0]
    exposures = psf.shape[3]
    near = (near0, near1, near2)
    pad = side // 2
    t = lax.axis_index("tile")
    s = lax.axis_index("mc")
    h = lax.axis_index("filt")
    first = h * filters
    sigma = 1 - 2 * lax.rem(t, 2)
    partner = {"tile": t + sigma}
    ahead = {"tile": lax.rem(t + 2 * sigma + tiles, tiles)}
    behind = {"tile": lax.rem(t - 2 * sigma + tiles, tiles)}
    twin = {"mc": 1 - s}
    across = {"filt": 1 - h, "mc": 1 - s}

    def remote(src, dst, sem, f, to):
        return pltpu.make_async_remote_copy(
            src_ref=src,
            dst_ref=dst,
            send_sem=sem.at[0, f],
            recv_sem=sem.at[1, f],
            device_id=to,
            device_id_type=MESH,
        )

    ours = pl.ds(first, filters)
    kern_in = pltpu.make_async_copy(kern_hbm, kern, tab_sem.at[0])
    psf_in = pltpu.make_async_copy(psf_hbm.at[ours], psf_b, tab_sem.at[1])
    inter_in = pltpu.make_async_copy(inter_hbm.at[ours], inter, tab_sem.at[2])
    count_in = pltpu.make_async_copy(count_hbm, count, tab_sem.at[3])
    prec_in = pltpu.make_async_copy(prec_hbm, prec, tab_sem.at[4])
    basis_move = pltpu.make_async_copy(basis_v, per_basis, tab_sem.at[6])
    psf_move = pltpu.make_async_copy(psf_f, psf, tab_sem.at[5])
    for copy in (kern_in, psf_in, inter_in, count_in, prec_in):
        copy.start()
    loads = []
    for f in range(filters):
        loads.append(
            [
                pltpu.make_async_copy(noise_hbm.at[f], noise.at[s, f], in_sem.at[0, f]),
                pltpu.make_async_copy(mean_hbm.at[f], mean.at[f], in_sem.at[1, f]),
                pltpu.make_async_copy(lsc_hbm.at[f], scale.at[f], in_sem.at[2, f]),
            ]
        )
    late = [
        pltpu.make_async_copy(obs_hbm, obs, in_sem.at[3, 0]),
        pltpu.make_async_copy(ivar_hbm, ivar, in_sem.at[3, 1]),
    ]
    for group in loads:
        for copy in group:
            copy.start()
    for copy in late:
        copy.start()

    barrier = pltpu.get_barrier_semaphore()
    for to in (partner, ahead, behind, twin, across):
        pl.semaphore_signal(barrier, inc=1, device_id=to, device_id_type=MESH)

    centre_i = lax.broadcasted_iota(jnp.int32, (STRIP, 128), 0)
    lrow[...] = (2 * centre_i + 1 - side).astype(F32) * (1.0 / side)
    centre_j = lax.broadcasted_iota(jnp.int32, (1, side), 1)
    lcol = (2 * centre_j + 1 - side).astype(F32) * (1.0 / side)
    lanes = lax.broadcasted_iota(jnp.int32, (1, 128), 1)
    placed[K] = jnp.zeros((side, side), BF16)
    edge = jnp.zeros((pad, 128), F32)

    def clear_edges(ref, at):
        for lo in range(2):
            ref[at, lo, 0:pad, :] = edge
            ref[at, lo, pad + side : side + 2 * pad, :] = edge

    for q in range(K):
        clear_edges(turn, q)

    kern_in.wait()
    taps[...] = jnp.zeros_like(taps)
    ntaps = kern.shape[2]
    for k in range(nbasis):
        taps[2 * k : 2 * k + 2, 0:ntaps] = kern[k]
    swap_i = lax.broadcasted_iota(jnp.int32, (128, 128), 0)
    swap_j = lax.broadcasted_iota(jnp.int32, (128, 128), 1)
    swap = jnp.where(swap_i + swap_j == ntaps - 1, 1.0, 0.0).astype(BF16)
    taps[2 * nbasis : 4 * nbasis, :] = dot(taps[0 : 2 * nbasis, :].astype(BF16), swap)

    def build(dst, from_row, stride, flat):
        def one(k, carry):
            row = taps[pl.ds(from_row + stride * k, 1), :]
            pat = jnp.broadcast_to(row, (16, 128))
            pat = pltpu.roll(pat, 0, 1, stride=1, stride_axis=0)
            for a in range(side // 16):
                left, right = band_rows(pat, a, side)
                for part, lo in ((left, 0), (right, 128)):
                    if flat:
                        at = pl.ds(pl.multiple_of(k * side + 16 * a, 16), 16)
                        dst[at, lo : lo + 128] = part.astype(BF16)
                    else:
                        dst[k, 16 * a : 16 * a + 16, lo : lo + 128] = part.astype(BF16)
            return carry

        lax.fori_loop(0, nbasis, one, 0)

    build(rmat, 2 * nbasis, 2, True)
    build(cmat_t, 1, 2, False)
    psf_in.wait()
    psf_f[...] = psf_b[...].astype(F32)
    psf_move.start()

    for f in range(filters):
        loads[f][0].wait()
    pl.semaphore_wait(barrier, 5)
    noise_out = remote(noise.at[s], noise.at[s], noise_sem, 0, twin)
    noise_out.start()

    def over_rows(body, chunk=32):
        def one(r, carry):
            body(pl.multiple_of(r * chunk, chunk), chunk)
            return carry

        lax.fori_loop(0, side // chunk, one, 0)

    inter_in.wait()
    count_in.wait()
    prec_in.wait()
    psf_move.wait()

    def slot_live(f, q):
        return q < count[first + f, t]

    def slot_exposure(f, q):
        return jnp.clip(inter[f, 0, q, t], 0, exposures - 1)

    def slot_coef(f, q):
        live = slot_live(f, q)
        e = slot_exposure(f, q)
        return [[jnp.where(live, psf[f, b, m, e], 0.0) for m in range(3)] for b in range(NB)]

    def lane_shift(by):
        whole = jnp.right_shift(by, 7)
        rest = jnp.bitwise_and(by, 127)
        right = lanes >= rest
        same = ((whole == 0) & right) | ((whole == -1) & ~right)
        from_high = (whole == -1) & right
        from_low = ((whole == 0) & ~right) | (whole == 1)

        def apply(low, high):
            low = pltpu.roll(low, rest, 1)
            high = pltpu.roll(high, rest, 1)
            none = jnp.zeros_like(low)
            return (
                jnp.where(same, low, jnp.where(from_high, high, none)),
                jnp.where(same, high, jnp.where(from_low, low, none)),
            )

        return apply

    def first_weight(constant, coef, lo):
        return (constant + coef[1] * lrow[...]) + coef[2] * lcol[:, 128 * lo : 128 * lo + 128]

    def forward(f):
        def sample_rows(r, n):
            rows = pl.ds(r, n)
            sc = jnp.exp(scale[f, rows, :])
            scale[f, rows, :] = sc
            x_ref[rows, :] = (mean[f, rows, :] + sc * noise[s, f, rows, :].astype(F32)).astype(BF16)

        over_rows(sample_rows)

        half_blur[...] = dot(rmat[...], x_ref[...]).astype(BF16)
        for k in range(nbasis):
            image = dot(half_blur[k * side : (k + 1) * side, :], cmat_t[k])
            blur[k, 0] = image[:, 0:128]
            blur[k, 1] = image[:, 128:256]

        def slot(q, carry):
            coef = slot_coef(f, q)
            oy = inter[f, 1, q, t]
            ox = inter[f, 2, q, t]
            kb = [inter[f, 3 + b, q, t] for b in range(NB)]
            up = oy.astype(F32) * (2.0 / side)
            over = ox.astype(F32) * (2.0 / side)
            c0 = [coef[b][0] + coef[b][1] * up + coef[b][2] * over for b in range(NB)]
            weight = [[first_weight(c0[b], coef[b], lo) for lo in range(2)] for b in range(NB)]
            step = [coef[b][1] * (2.0 * STRIP / side) for b in range(NB)]
            move = lane_shift(ox)

            def mix_rows(i, weight):
                r = pl.multiple_of(i * STRIP, STRIP)
                for lo in range(2):
                    acc = None
                    for b in range(NB):
                        term = weight[b][lo] * blur[kb[b], lo, pl.ds(r, STRIP), :]
                        acc = term if acc is None else acc + term
                    turn[q, lo, pl.ds(pad + r, STRIP), :] = acc
                return [[weight[b][lo] + step[b] for lo in range(2)] for b in range(NB)]

            lax.fori_loop(0, side // STRIP, mix_rows, weight, unroll=4)

            def place_rows(r, n):
                low, high = move(*[turn[q, lo, pl.ds(pad - oy + r, n), :] for lo in range(2)])
                placed[q, pl.ds(r, n), 0:128] = low.astype(BF16)
                placed[q, pl.ds(r, n), 128:256] = high.astype(BF16)

            over_rows(place_rows, 64)
            return carry

        lax.fori_loop(0, K, slot, 0)
        place = [jnp.where(slot_live(f, q), inter[f, 0, q, t] - t, WINDOW) for q in range(K)]

        def pick(d):
            at = K
            for q in range(K):
                at = jnp.where(place[q] == d, q, at)
            return placed[at]

        own[f] = pick(0)
        send_p[f, 0] = pick(sigma)
        send_p[f, 1] = pick(-sigma)
        send_d[f] = pick(-2 * sigma)
        send_q[f] = pick(2 * sigma)

    def p_copy(f):
        return remote(send_p.at[f], recv_p.at[f], p_sem, f, partner)

    def d_copy(f):
        return remote(send_d.at[f], recv_d.at[f], d_sem, f, behind)

    def q_copy(f):
        return remote(send_q.at[f], recv_q.at[f], q_sem, f, ahead)

    def merge(f):
        p_copy(f).wait_recv()

        def rows_of(r, n):
            rows = pl.ds(r, n)
            joined = send_q[f, rows, :].astype(F32) + recv_p[f, 1, rows, :].astype(F32)
            send_q[f, rows, :] = joined.astype(BF16)

        over_rows(rows_of)
        q_copy(f).start()

    for f in range(filters):
        loads[f][1].wait()
        loads[f][2].wait()
        forward(f)
        p_copy(f).start()
        d_copy(f).start()
        if f > 0:
            merge(f - 1)
    merge(filters - 1)

    noise_out.wait_recv()

    def g_copy(f):
        return remote(send_g.at[f], recv_g.at[f], g_sem, f, across)

    for f in range(filters):

        def twin_rows(r, n):
            rows = pl.ds(r, n)
            other = noise[1 - s, f, rows, :].astype(F32)
            send_g[f, rows, :] = (mean[f, rows, :] + scale[f, rows, :] * other).astype(BF16)

        over_rows(twin_rows)
        g_copy(f).start()

    build(rmat_t, 0, 2, False)
    build(cmat, 2 * nbasis + 1, 2, True)

    def rp_copy(f):
        return remote(near[f].at[REACH], near[f].at[REACH - sigma], rp_sem, f, partner)

    def ru_copy(f):
        return remote(near[f].at[REACH], near[f].at[REACH - 2 * sigma], ru_sem, f, ahead)

    def rd_copy(f):
        return remote(near[f].at[REACH], near[f].at[REACH + 2 * sigma], rd_sem, f, behind)

    def relay_copy(f):
        return remote(near[f].at[REACH + 2 * sigma], near[f].at[REACH + sigma], relay_sem, f, partner)

    for copy in late:
        copy.wait()

    def residual(f):
        d_copy(f).wait_recv()
        q_copy(f).wait_recv()

        def rows_of(r, n):
            rows = pl.ds(r, n)
            pred = own[f, rows, :].astype(F32) + recv_p[f, 0, rows, :].astype(F32)
            pred = pred + recv_d[f, rows, :].astype(F32) + recv_q[f, rows, :].astype(F32)
            res = ivar[f, rows, :].astype(F32) * (obs[f, rows, :].astype(F32) - pred)
            near[f][REACH, rows, :] = res.astype(BF16)

        over_rows(rows_of)
        ru_copy(f).start()
        rd_copy(f).start()
        rp_copy(f).start()

    def basis_table(fq, carry):
        f = fq // K
        q = fq - K * f
        coef = slot_coef(f, q)
        up = inter[f, 1, q, t].astype(F32) * (2.0 / side)
        across_by = inter[f, 2, q, t].astype(F32) * (2.0 / side)
        kb = [inter[f, 3 + b, q, t] for b in range(NB)]
        for b in range(NB):
            coef[b][0] = coef[b][0] + coef[b][1] * up + coef[b][2] * across_by
        for m in range(3):
            total = jnp.zeros((1, 128), F32)
            for b in range(NB):
                total = total + jnp.where(lanes == kb[b], coef[b][m], 0.0)
            basis_v[pl.ds(3 * fq + m, 1), :] = total
        return carry

    def own_prior():
        rows_in = [[prec[first + f, first + g] for g in range(filters)] for f in range(filters)]

        def rows_of(r, n):
            rows = pl.ds(r, n)
            sam = [[None] * filters for _ in range(2)]
            dev = [[None] * filters for _ in range(2)]
            for g in range(filters):
                mn, sc = mean[g, rows, :], scale[g, rows, :]
                for which in range(2):
                    dev[which][g] = sc * noise[which, g, rows, :].astype(F32)
                    sam[which][g] = mn + dev[which][g]
            for f in range(filters):
                pri = []
                for which in range(2):
                    total = None
                    for g in range(filters):
                        term = rows_in[f][g] * sam[which][g]
                        total = term if total is None else total + term
                    pri.append(total)
                pri_mu[f, rows, :] = pri[0] + pri[1]
                pri_rho[f, rows, :] = pri[0] * dev[0][f] + pri[1] * dev[1][f]

        over_rows(rows_of, 16)

    def e_copy(f):
        return remote(e_ref.at[s, f], e_ref.at[s, f], e_sem, f, twin)

    def backward(f):
        ru_copy(f).wait_recv()
        rp_copy(f).wait_recv()
        relay_copy(f).wait_recv()

        def pull(q, carry):
            at = jnp.clip(inter[f, 0, q, t] - t + REACH, 0, WINDOW - 1)
            move = lane_shift(-inter[f, 2, q, t])

            def pull_rows(r, n):
                image = near[f][at, pl.ds(r, n), :].astype(F32)
                low, high = move(image[:, 0:128], image[:, 128:256])
                turn[q, 0, pl.ds(pad + r, n), :] = low
                turn[q, 1, pl.ds(pad + r, n), :] = high

            over_rows(pull_rows, 64)
            oy = inter[f, 1, q, t]

            def settle_rows(r, n):
                for lo in range(2):
                    moved[q, lo, pl.ds(r, n), :] = turn[q, lo, pl.ds(pad + oy + r, n), :]

            over_rows(settle_rows, 64)
            return carry

        lax.fori_loop(0, K, pull, 0)

        def weigh(k, dst):
            coef = [[per_basis[(f * K + q) * 3 + m, k] for m in range(3)] for q in range(K)]
            weight = [[first_weight(coef[q][0], coef[q], lo) for lo in range(2)] for q in range(K)]
            step = [coef[q][1] * (2.0 * STRIP / side) for q in range(K)]
            for r in range(0, side, STRIP):
                for lo in range(2):
                    acc = None
                    for q in range(K):
                        term = weight[q][lo] * moved[q, lo, r : r + STRIP, :]
                        acc = term if acc is None else acc + term
                        if r + STRIP < side:
                            weight[q][lo] = weight[q][lo] + step[q]
                    dst[r : r + STRIP, 128 * lo : 128 * lo + 128] = acc.astype(BF16)

        def pull_back(k, src):
            at = pl.ds(pl.multiple_of(k * side, side), side)
            half[:, at] = dot(rmat_t[k], src[...]).astype(BF16)

        weigh(0, x_ref)

        def pair(j, carry):
            weigh(2 * j + 1, y_ref)
            pull_back(2 * j, x_ref)
            weigh(2 * j + 2, x_ref)
            pull_back(2 * j + 1, y_ref)
            return carry

        lax.fori_loop(0, nbasis // 2 - 1, pair, 0)
        weigh(nbasis - 1, y_ref)
        pull_back(nbasis - 2, x_ref)
        pull_back(nbasis - 1, y_ref)
        others = (1 - h) * filters
        cross = [prec[first + f, others + g] for g in range(filters)]
        grad = dot(half[...], cmat[...])
        for g in range(filters):
            grad = grad - cross[g] * recv_g[g].astype(F32)
        e_ref[s, f] = grad.astype(BF16)
        e_copy(f).start()

    def final(f):
        e_copy(f).wait_recv()

        def rows_of(r, n):
            rows = pl.ds(r, n)
            sc = scale[f, rows, :]
            e0 = e_ref[0, f, rows, :].astype(F32)
            e1 = e_ref[1, f, rows, :].astype(F32)
            d0 = sc * noise[0, f, rows, :].astype(F32)
            d1 = sc * noise[1, f, rows, :].astype(F32)
            mu[f, rows, :] = 0.5 * ((e0 + e1) - pri_mu[f, rows, :])
            rho[f, rows, :] = 0.5 * ((e0 * d0 + e1 * d1) - pri_rho[f, rows, :]) + 1.0

        over_rows(rows_of)

    def relay(f):
        rd_copy(f).wait_recv()
        relay_copy(f).start()

    residual(0)
    lax.fori_loop(0, filters * K, basis_table, 0)
    basis_move.start()
    residual(1)
    own_prior()
    residual(2)
    basis_move.wait()
    relay(0)
    for f in range(filters):
        g_copy(f).wait_recv()
    backward(0)
    relay(1)
    backward(1)
    final(0)
    relay(2)
    backward(2)
    final(1)
    final(2)

    noise_out.wait_send()
    for f in range(filters):
        for copy in (p_copy, d_copy, q_copy, g_copy, ru_copy, rd_copy, rp_copy, relay_copy, e_copy):
            copy(f).wait_send()


def body(tiles, sky_mean, sky_log_scale, noise_draw, observed, inv_var, intersections, counts, kernels, psf_coeffs, prior_prec):
    filters, side = sky_mean.shape[1], sky_mean.shape[2]
    nbasis, _, taps = kernels.shape
    every, fields = intersections.shape[1], intersections.shape[3]
    exposures = psf_coeffs.shape[0]
    img = (side, side)
    padded = (2, 2 * side, 128)
    vmem = pltpu.VMEM
    smem = pltpu.SMEM
    dma = pltpu.SemaphoreType.DMA
    mu, rho = pl.pallas_call(
        functools.partial(kernel, tiles),
        out_shape=[jax.ShapeDtypeStruct((filters,) + img, F32)] * 2,
        in_specs=[pl.BlockSpec(memory_space=pltpu.HBM)] * 10,
        out_specs=[pl.BlockSpec(memory_space=pltpu.VMEM)] * 2,
        scratch_shapes=[
            vmem((nbasis, 2, taps), F32),
            vmem((4 * nbasis, 128), F32),
            smem((filters, fields, K, intersections.shape[0]), jnp.int32),
            smem((every, counts.shape[0]), jnp.int32),
            vmem((filters, NB, 3, exposures), BF16),
            vmem((filters, NB, 3, exposures), F32),
            smem((filters, NB, 3, exposures), F32),
            smem((every, every), F32),
            vmem((filters * K * 3, 128), F32),
            smem((filters * K * 3, 128), F32),
            vmem((filters,) + img, F32),
            vmem((filters,) + img, F32),
            vmem((2, filters) + img, BF16),
            vmem((filters,) + img, BF16),
            vmem((filters,) + img, BF16),
            vmem((STRIP, 128), F32),
            vmem((nbasis * side, side), BF16),
            vmem((nbasis,) + img, BF16),
            vmem((nbasis * side, side), BF16),
            vmem((nbasis,) + img, BF16),
            vmem(img, BF16),
            vmem(img, BF16),
            vmem((nbasis * side, side), BF16),
            vmem((nbasis, 2, side, 128), F32),
            vmem((K,) + padded, F32),
            vmem((K + 1,) + img, BF16),
            vmem((filters,) + img, BF16),
            vmem((filters, 2) + img, BF16),
            vmem((filters, 2) + img, BF16),
            vmem((filters,) + img, BF16),
            vmem((filters,) + img, BF16),
            vmem((filters,) + img, BF16),
            vmem((filters,) + img, BF16),
            vmem((WINDOW,) + img, BF16),
            vmem((WINDOW,) + img, BF16),
            vmem((WINDOW,) + img, BF16),
            vmem((K, 2, side, 128), F32),
            vmem((side, nbasis * side), BF16),
            vmem((filters,) + img, BF16),
            vmem((filters,) + img, BF16),
            vmem((2, filters) + img, BF16),
            vmem((filters,) + img, F32),
            vmem((filters,) + img, F32),
            dma((4, filters)),
            dma((7,)),
            dma((2, 1)),
        ]
        + [dma((2, filters))] * 9,
        compiler_params=pltpu.CompilerParams(
            collective_id=0, has_side_effects=True, vmem_limit_bytes=60 * 1024 * 1024
        ),
    )(
        kernels,
        jnp.transpose(intersections, (1, 3, 2, 0)),
        jnp.transpose(counts),
        jnp.transpose(psf_coeffs, (1, 2, 3, 0)),
        prior_prec,
        sky_mean[0],
        sky_log_scale[0],
        noise_draw[0, 0],
        observed[0],
        inv_var[0],
    )
    return mu[None], rho[None]


def solution(mesh):
    placed = (
        P("tile", "filt", None, None),
        P("tile", "filt", None, None),
        P("mc", "tile", "filt", None, None),
        P("tile", "filt", None, None),
        P("tile", "filt", None, None),
        P(),
        P(),
        P(),
        P(),
        P(),
    )
    return jax.shard_map(
        functools.partial(body, mesh.shape["tile"]),
        mesh=mesh,
        in_specs=placed,
        out_specs=(P("tile", "filt", None, None), P("tile", "filt", None, None)),
        check_vma=False,
    )
```

time: 75.2 us -> 57.9 us (0.77)
  local copies, waits for them, and re-layouts: 10 us -> 3.02 us
  Pallas kernels: 60.4 us -> 54 us
  other arithmetic: 3.62 us -> 0 us
    pallas_call x1, Pallas kernels: 60.4 us -> 54 us  [body(): pl.pallas_call(functools.partial(kernel, tiles), out_shape=[jax.ShapeDtyp...]
    unnamed x14 -> x4, local copies, waits for them, and re-layouts: 5.9 us -> 3.02 us
    dynamic_slice x4 -> x0, local copies, waits for them, and re-layouts: 1.89 us -> none  [the longest x1 0.95 us: tables(): lax.dynamic_slice(counts, (tile_here, first), (1, local_filters))[0]]
    select_n x2 -> x0, other arithmetic: 1.2 us -> none  [the longest x1 0.76 us: tables(): jnp.where(first > 0, jnp.concatenate([prec[:, local_filters:], prec[:, :l...]
    transpose x1 -> x0, other arithmetic: 0.8 us -> none  [tables(): jnp.transpose(psf, (1, 0, 2, 3))[:, None]]
    concatenate x2 -> x0, other arithmetic: 0.78 us -> none  [the longest x1 0.7 us: body(): jnp.concatenate([flat, flat[:, ::-1]], 0)]
    rev x1 -> x0, local copies, waits for them, and re-layouts: 0.77 us -> none  [body(): flat[:, ::-1]]
where the time goes in v2:
time: 57.9 us; the launch traced here: 57.7 us
  Pallas kernels  54 us (93%)
  local copies, waits for them, and re-layouts  3.02 us (5%)
  between operations  0.65 us (1%)
    pallas_call x1, Pallas kernels, body(): pl.pallas_call(functools.partial(kernel, tiles), out_shape=[jax.ShapeDtyp...  54 us
    unnamed x4, local copies, waits for them, and re-layouts  3.02 us

profile of v2, /device:TPU:1, one launch (start us, length us, event | category | flops | bytes accessed | tf_op | source)
XLA Modules:
  0.0 57.7 jit_solution(639763459453917718)
XLA Ops:
  0.6 54.0 %shard_map.113 = (f32[3,256,256]{2,1,0:T(8,128)}, f32[3,256,256]{2,1,0:T(8,128)}) custom-call(f32[8,2,25]{2,1,0:T(2,128)} %kern_hbm.1, s32[6,9,3,128]{3,2,1,0:T(4,128)} %bitcast.17, s32[6,128]{1,0:T(8,128)} %bitcast.19, bf16[6,6,3,128]{3,2,1,0:T(4,128)(2,1)} %bitcast.18, f32[6,6]{1,0:T(8,128)} %prec_hbm.1, f32[3,256,256]{2,1,0:T(8,128)} %bitcast.12, ...), custom_call_target="tpu_custom_call" | custom-call | tf_op jit(solution)/shard_map/pallas_call | solution.py:578
  54.7 0.0 copy-start
  54.7 2.1 %copy.14 = f32[1,3,256,256]{3,2,1,0:T(8,128)} copy(f32[1,3,256,256]{3,2,1,0:T(8,128)} %bitcast.11) | data formatting | bytes 1572864
  56.8 0.0 copy-done
  56.8 0.9 %copy.15 = f32[1,3,256,256]{3,2,1,0:T(8,128)} copy(f32[1,3,256,256]{3,2,1,0:T(8,128)S(1)} %bitcast.10) | data formatting | bytes 1572864
Async XLA Ops:
  54.7 2.1 %copy-start = (f32[3,256,256]{2,1,0:T(8,128)S(1)}, f32[3,256,256]{2,1,0:T(8,128)}, u32[]{:S(2)}) copy-start(f32[3,256,256]{2,1,0:T(8,128)} %get-tuple-element.5) | copy-start | bytes 2359300

commit v3 on v2

--- a/solution.py
+++ b/solution.py
@@ -186,6 +186,15 @@
     for q in range(K):
         clear_edges(turn, q)
 
+    def noise_copy(f):
+        return remote(noise.at[s, f], noise.at[s, f], noise_sem, f, twin)
+
+    for f in range(filters):
+        loads[f][0].wait()
+    pl.semaphore_wait(barrier, 5)
+    for f in range(filters):
+        noise_copy(f).start()
+
     kern_in.wait()
     taps[...] = jnp.zeros_like(taps)
     ntaps = kern.shape[2]
@@ -219,12 +228,6 @@
     psf_f[...] = psf_b[...].astype(F32)
     psf_move.start()
 
-    for f in range(filters):
-        loads[f][0].wait()
-    pl.semaphore_wait(barrier, 5)
-    noise_out = remote(noise.at[s], noise.at[s], noise_sem, 0, twin)
-    noise_out.start()
-
     def over_rows(body, chunk=32):
         def one(r, carry):
             body(pl.multiple_of(r * chunk, chunk), chunk)
@@ -352,22 +355,11 @@
         over_rows(rows_of)
         q_copy(f).start()
 
-    for f in range(filters):
-        loads[f][1].wait()
-        loads[f][2].wait()
-        forward(f)
-        p_copy(f).start()
-        d_copy(f).start()
-        if f > 0:
-            merge(f - 1)
-    merge(filters - 1)
-
-    noise_out.wait_recv()
-
     def g_copy(f):
         return remote(send_g.at[f], recv_g.at[f], g_sem, f, across)
 
-    for f in range(filters):
+    def twin_sample(f):
+        noise_copy(f).wait_recv()
 
         def twin_rows(r, n):
             rows = pl.ds(r, n)
@@ -377,9 +369,6 @@
         over_rows(twin_rows)
         g_copy(f).start()
 
-    build(rmat_t, 0, 2, False)
-    build(cmat, 2 * nbasis + 1, 2, True)
-
     def rp_copy(f):
         return remote(near[f].at[REACH], near[f].at[REACH - sigma], rp_sem, f, partner)
 
@@ -391,9 +380,6 @@
 
     def relay_copy(f):
         return remote(near[f].at[REACH + 2 * sigma], near[f].at[REACH + sigma], relay_sem, f, partner)
-
-    for copy in late:
-        copy.wait()
 
     def residual(f):
         d_copy(f).wait_recv()
@@ -513,6 +499,9 @@
         weigh(nbasis - 1, y_ref)
         pull_back(nbasis - 2, x_ref)
         pull_back(nbasis - 1, y_ref)
+        if f == 0:
+            for g in range(filters):
+                g_copy(g).wait_recv()
         others = (1 - h) * filters
         cross = [prec[first + f, others + g] for g in range(filters)]
         grad = dot(half[...], cmat[...])
@@ -540,16 +529,34 @@
         rd_copy(f).wait_recv()
         relay_copy(f).start()
 
+    def start_forward(f):
+        loads[f][1].wait()
+        loads[f][2].wait()
+        forward(f)
+        p_copy(f).start()
+        d_copy(f).start()
+
+    start_forward(0)
+    start_forward(1)
+    merge(0)
+    twin_sample(0)
+    start_forward(2)
+    merge(1)
+    for copy in late:
+        copy.wait()
+    twin_sample(1)
+    merge(2)
     residual(0)
     lax.fori_loop(0, filters * K, basis_table, 0)
     basis_move.start()
+    build(rmat_t, 0, 2, False)
     residual(1)
+    build(cmat, 2 * nbasis + 1, 2, True)
+    twin_sample(2)
     own_prior()
     residual(2)
     basis_move.wait()
     relay(0)
-    for f in range(filters):
-        g_copy(f).wait_recv()
     backward(0)
     relay(1)
     backward(1)
@@ -559,9 +566,8 @@
     final(1)
     final(2)
 
-    noise_out.wait_send()
     for f in range(filters):
-        for copy in (p_copy, d_copy, q_copy, g_copy, ru_copy, rd_copy, rp_copy, relay_copy, e_copy):
+        for copy in (noise_copy, p_copy, d_copy, q_copy, g_copy, ru_copy, rd_copy, rp_copy, relay_copy, e_copy):
             copy(f).wait_send()
 
 
@@ -626,23 +632,27 @@
             vmem((filters,) + img, F32),
             dma((4, filters)),
             dma((7,)),
-            dma((2, 1)),
-        ]
-        + [dma((2, filters))] * 9,
+            ]
+        + [dma((2, filters))] * 10,
         compiler_params=pltpu.CompilerParams(
-            collective_id=0, has_side_effects=True, vmem_limit_bytes=60 * 1024 * 1024
+            collective_id=0, has_side_effects=True, vmem_limit_bytes=48 * 1024 * 1024
         ),
     )(
-        kernels,
-        jnp.transpose(intersections, (1, 3, 2, 0)),
-        jnp.transpose(counts),
-        jnp.transpose(psf_coeffs, (1, 2, 3, 0)),
-        prior_prec,
-        sky_mean[0],
-        sky_log_scale[0],
-        noise_draw[0, 0],
-        observed[0],
-        inv_var[0],
+        *[
+            pltpu.with_memory_space_constraint(value, pltpu.HBM)
+            for value in (
+                kernels,
+                jnp.transpose(intersections, (1, 3, 2, 0)),
+                jnp.transpose(counts),
+                jnp.transpose(psf_coeffs, (1, 2, 3, 0)),
+                prior_prec,
+                sky_mean[0],
+                sky_log_scale[0],
+                noise_draw[0, 0],
+                observed[0],
+                inv_var[0],
+            )
+        ]
     )
     return mu[None], rho[None]
 

time: 57.9 us -> 56.5 us (0.976)
  local copies, waits for them, and re-layouts: 3.02 us -> 1.76 us
    unnamed x4 -> x2, local copies, waits for them, and re-layouts: 3.02 us -> 1.76 us
where the time goes in v3:
time: 56.5 us; the launch traced here: 56.4 us
  Pallas kernels  54 us (96%)
  local copies, waits for them, and re-layouts  1.76 us (3%)
  between operations  0.64 us (1%)
    pallas_call x1, Pallas kernels, body(): pl.pallas_call(functools.partial(kernel, tiles), out_shape=[jax.ShapeDtyp...  54 us
    unnamed x2, local copies, waits for them, and re-layouts  1.76 us

profile of v3, /device:TPU:1, one launch (start us, length us, event | category | flops | bytes accessed | tf_op | source)
XLA Modules:
  0.0 56.4 jit_solution(3590934407990149416)
XLA Ops:
  0.6 54.0 %shard_map.113 = (f32[3,256,256]{2,1,0:T(8,128)S(1)}, f32[3,256,256]{2,1,0:T(8,128)S(1)}) custom-call(f32[8,2,25]{2,1,0:T(2,128)} %kern_hbm.1, s32[6,9,3,128]{3,2,1,0:T(4,128)} %bitcast.17, s32[6,128]{1,0:T(8,128)} %bitcast.19, bf16[6,6,3,128]{3,2,1,0:T(4,128)(2,1)} %bitcast.18, f32[6,6]{1,0:T(8,128)} %prec_hbm.1, f32[3,256,256]{2,1,0:T(8,128)} %bitcast.12, ...), custom_call_target="tpu_custom_call" | custom-call | tf_op jit(solution)/shard_map/pallas_call | solution.py:584
  54.6 0.9 %copy.14 = f32[1,3,256,256]{3,2,1,0:T(8,128)} copy(f32[1,3,256,256]{3,2,1,0:T(8,128)S(1)} %bitcast.11) | data formatting | bytes 1572864
  55.5 0.9 %copy.15 = f32[1,3,256,256]{3,2,1,0:T(8,128)} copy(f32[1,3,256,256]{3,2,1,0:T(8,128)S(1)} %bitcast.10) | data formatting | bytes 1572864

commit v4 on v3

--- a/solution.py
+++ b/solution.py
@@ -229,11 +229,8 @@
     psf_move.start()
 
     def over_rows(body, chunk=32):
-        def one(r, carry):
-            body(pl.multiple_of(r * chunk, chunk), chunk)
-            return carry
-
-        lax.fori_loop(0, side // chunk, one, 0)
+        for r in range(0, side, chunk):
+            body(r, chunk)
 
     inter_in.wait()
     count_in.wait()
@@ -273,7 +270,7 @@
     def first_weight(constant, coef, lo):
         return (constant + coef[1] * lrow[...]) + coef[2] * lcol[:, 128 * lo : 128 * lo + 128]
 
-    def forward(f):
+    def forward(f, between):
         def sample_rows(r, n):
             rows = pl.ds(r, n)
             sc = jnp.exp(scale[f, rows, :])
@@ -287,6 +284,8 @@
             image = dot(half_blur[k * side : (k + 1) * side, :], cmat_t[k])
             blur[k, 0] = image[:, 0:128]
             blur[k, 1] = image[:, 128:256]
+
+        between()
 
         def slot(q, carry):
             coef = slot_coef(f, q)
@@ -301,7 +300,7 @@
             move = lane_shift(ox)
 
             def mix_rows(i, weight):
-                r = pl.multiple_of(i * STRIP, STRIP)
+                r = i * STRIP
                 for lo in range(2):
                     acc = None
                     for b in range(NB):
@@ -310,17 +309,20 @@
                     turn[q, lo, pl.ds(pad + r, STRIP), :] = acc
                 return [[weight[b][lo] + step[b] for lo in range(2)] for b in range(NB)]
 
-            lax.fori_loop(0, side // STRIP, mix_rows, weight, unroll=4)
+            for i in range(side // STRIP):
+                weight = mix_rows(i, weight)
 
             def place_rows(r, n):
                 low, high = move(*[turn[q, lo, pl.ds(pad - oy + r, n), :] for lo in range(2)])
                 placed[q, pl.ds(r, n), 0:128] = low.astype(BF16)
                 placed[q, pl.ds(r, n), 128:256] = high.astype(BF16)
 
-            over_rows(place_rows, 64)
+            for r in range(0, side, 64):
+                place_rows(r, 64)
             return carry
 
-        lax.fori_loop(0, K, slot, 0)
+        for q in range(K):
+            slot(q, 0)
         place = [jnp.where(slot_live(f, q), inter[f, 0, q, t] - t, WINDOW) for q in range(K)]
 
         def pick(d):
@@ -441,7 +443,7 @@
     def e_copy(f):
         return remote(e_ref.at[s, f], e_ref.at[s, f], e_sem, f, twin)
 
-    def backward(f):
+    def backward(f, between):
         ru_copy(f).wait_recv()
         rp_copy(f).wait_recv()
         relay_copy(f).wait_recv()
@@ -466,7 +468,8 @@
             over_rows(settle_rows, 64)
             return carry
 
-        lax.fori_loop(0, K, pull, 0)
+        for q in range(K):
+            pull(q, 0)
 
         def weigh(k, dst):
             coef = [[per_basis[(f * K + q) * 3 + m, k] for m in range(3)] for q in range(K)]
@@ -483,8 +486,7 @@
                     dst[r : r + STRIP, 128 * lo : 128 * lo + 128] = acc.astype(BF16)
 
         def pull_back(k, src):
-            at = pl.ds(pl.multiple_of(k * side, side), side)
-            half[:, at] = dot(rmat_t[k], src[...]).astype(BF16)
+            half[:, k * side : (k + 1) * side] = dot(rmat_t[k], src[...]).astype(BF16)
 
         weigh(0, x_ref)
 
@@ -495,7 +497,9 @@
             pull_back(2 * j + 1, y_ref)
             return carry
 
-        lax.fori_loop(0, nbasis // 2 - 1, pair, 0)
+        for j in range(nbasis // 2 - 1):
+            pair(j, 0)
+        between()
         weigh(nbasis - 1, y_ref)
         pull_back(nbasis - 2, x_ref)
         pull_back(nbasis - 1, y_ref)
@@ -529,40 +533,42 @@
         rd_copy(f).wait_recv()
         relay_copy(f).start()
 
-    def start_forward(f):
+    def start_forward(f, between):
         loads[f][1].wait()
         loads[f][2].wait()
-        forward(f)
+        forward(f, between)
         p_copy(f).start()
         d_copy(f).start()
 
-    start_forward(0)
-    start_forward(1)
-    merge(0)
-    twin_sample(0)
-    start_forward(2)
-    merge(1)
+    def nothing():
+        pass
+
+    def between_last():
+        merge(1)
+        twin_sample(0)
+
+    start_forward(0, nothing)
+    start_forward(1, lambda: merge(0))
+    start_forward(2, between_last)
     for copy in late:
         copy.wait()
+    residual(0)
     twin_sample(1)
     merge(2)
-    residual(0)
     lax.fori_loop(0, filters * K, basis_table, 0)
     basis_move.start()
+    residual(1)
+    twin_sample(2)
     build(rmat_t, 0, 2, False)
-    residual(1)
     build(cmat, 2 * nbasis + 1, 2, True)
-    twin_sample(2)
+    residual(2)
     own_prior()
-    residual(2)
     basis_move.wait()
     relay(0)
-    backward(0)
-    relay(1)
-    backward(1)
+    backward(0, lambda: relay(1))
+    backward(1, lambda: relay(2))
+    backward(2, nothing)
     final(0)
-    relay(2)
-    backward(2)
     final(1)
     final(2)
 

time: 56.5 us -> 51.9 us (0.919)
  Pallas kernels: 54 us -> 49.4 us
    pallas_call x1, Pallas kernels: 54 us -> 49.4 us  [body(): pl.pallas_call(functools.partial(kernel, tiles), out_shape=[jax.ShapeDtyp...]
where the time goes in v4:
time: 51.9 us; the launch traced here: 51.8 us
  Pallas kernels  49.4 us (95%)
  local copies, waits for them, and re-layouts  1.76 us (3%)
  between operations  0.64 us (1%)
    pallas_call x1, Pallas kernels, body(): pl.pallas_call(functools.partial(kernel, tiles), out_shape=[jax.ShapeDtyp...  49.4 us
    unnamed x2, local copies, waits for them, and re-layouts  1.76 us

profile of v4, /device:TPU:1, one launch (start us, length us, event | category | flops | bytes accessed | tf_op | source)
XLA Modules:
  0.0 51.8 jit_solution(11714084428564944565)
XLA Ops:
  0.6 49.4 %shard_map.113 = (f32[3,256,256]{2,1,0:T(8,128)S(1)}, f32[3,256,256]{2,1,0:T(8,128)S(1)}) custom-call(f32[8,2,25]{2,1,0:T(2,128)} %kern_hbm.1, s32[6,9,3,128]{3,2,1,0:T(4,128)} %bitcast.17, s32[6,128]{1,0:T(8,128)} %bitcast.19, bf16[6,6,3,128]{3,2,1,0:T(4,128)(2,1)} %bitcast.18, f32[6,6]{1,0:T(8,128)} %prec_hbm.1, f32[3,256,256]{2,1,0:T(8,128)} %bitcast.12, ...), custom_call_target="tpu_custom_call" | custom-call | tf_op jit(solution)/shard_map/pallas_call | solution.py:590
  50.0 0.9 %copy.14 = f32[1,3,256,256]{3,2,1,0:T(8,128)} copy(f32[1,3,256,256]{3,2,1,0:T(8,128)S(1)} %bitcast.11) | data formatting | bytes 1572864
  50.9 0.9 %copy.15 = f32[1,3,256,256]{3,2,1,0:T(8,128)} copy(f32[1,3,256,256]{3,2,1,0:T(8,128)S(1)} %bitcast.10) | data formatting | bytes 1572864

commit v5 on v4

--- a/solution.py
+++ b/solution.py
@@ -124,6 +124,8 @@
     partner = {"tile": t + sigma}
     ahead = {"tile": lax.rem(t + 2 * sigma + tiles, tiles)}
     behind = {"tile": lax.rem(t - 2 * sigma + tiles, tiles)}
+    has_ahead = (t + 2 * sigma >= 0) & (t + 2 * sigma < tiles)
+    has_behind = (t - 2 * sigma >= 0) & (t - 2 * sigma < tiles)
     twin = {"mc": 1 - s}
     across = {"filt": 1 - h, "mc": 1 - s}
 
@@ -167,8 +169,14 @@
         copy.start()
 
     barrier = pltpu.get_barrier_semaphore()
-    for to in (partner, ahead, behind, twin, across):
+
+    def greet(to):
         pl.semaphore_signal(barrier, inc=1, device_id=to, device_id_type=MESH)
+
+    for to in (partner, twin, across):
+        greet(to)
+    pl.when(has_ahead)(lambda: greet(ahead))
+    pl.when(has_behind)(lambda: greet(behind))
 
     centre_i = lax.broadcasted_iota(jnp.int32, (STRIP, 128), 0)
     lrow[...] = (2 * centre_i + 1 - side).astype(F32) * (1.0 / side)
@@ -191,9 +199,26 @@
 
     for f in range(filters):
         loads[f][0].wait()
-    pl.semaphore_wait(barrier, 5)
+    inner = has_ahead & has_behind
+    pl.when(inner)(lambda: pl.semaphore_wait(barrier, 5))
+    pl.when(jnp.logical_not(inner))(lambda: pl.semaphore_wait(barrier, 4))
     for f in range(filters):
         noise_copy(f).start()
+
+    blank = jnp.zeros((side, side), BF16)
+
+    @pl.when(jnp.logical_not(has_ahead))
+    def _():
+        for f in range(filters):
+            recv_d[f] = blank
+            near[f][REACH + 2 * sigma] = blank
+
+    @pl.when(jnp.logical_not(has_behind))
+    def _():
+        for f in range(filters):
+            recv_q[f] = blank
+            near[f][REACH - 2 * sigma] = blank
+            near[f][REACH - sigma] = blank
 
     kern_in.wait()
     taps[...] = jnp.zeros_like(taps)
@@ -207,35 +232,28 @@
 
     def build(dst, from_row, stride, flat):
         def one(k, carry):
-            row = taps[pl.ds(from_row + stride * k, 1), :]
+            row = taps[from_row + stride * k : from_row + stride * k + 1, :]
             pat = jnp.broadcast_to(row, (16, 128))
             pat = pltpu.roll(pat, 0, 1, stride=1, stride_axis=0)
             for a in range(side // 16):
                 left, right = band_rows(pat, a, side)
                 for part, lo in ((left, 0), (right, 128)):
                     if flat:
-                        at = pl.ds(pl.multiple_of(k * side + 16 * a, 16), 16)
+                        at = slice(k * side + 16 * a, k * side + 16 * a + 16)
                         dst[at, lo : lo + 128] = part.astype(BF16)
                     else:
                         dst[k, 16 * a : 16 * a + 16, lo : lo + 128] = part.astype(BF16)
             return carry
 
-        lax.fori_loop(0, nbasis, one, 0)
+        for k in range(nbasis):
+            one(k, 0)
 
     build(rmat, 2 * nbasis, 2, True)
     build(cmat_t, 1, 2, False)
-    psf_in.wait()
-    psf_f[...] = psf_b[...].astype(F32)
-    psf_move.start()
 
     def over_rows(body, chunk=32):
         for r in range(0, side, chunk):
             body(r, chunk)
-
-    inter_in.wait()
-    count_in.wait()
-    prec_in.wait()
-    psf_move.wait()
 
     def slot_live(f, q):
         return q < count[first + f, t]
@@ -279,6 +297,10 @@
 
         over_rows(sample_rows)
 
+        if f == 0:
+            psf_in.wait()
+            psf_f[...] = psf_b[...].astype(F32)
+            psf_move.start()
         half_blur[...] = dot(rmat[...], x_ref[...]).astype(BF16)
         for k in range(nbasis):
             image = dot(half_blur[k * side : (k + 1) * side, :], cmat_t[k])
@@ -355,7 +377,7 @@
             send_q[f, rows, :] = joined.astype(BF16)
 
         over_rows(rows_of)
-        q_copy(f).start()
+        pl.when(has_ahead)(lambda: q_copy(f).start())
 
     def g_copy(f):
         return remote(send_g.at[f], recv_g.at[f], g_sem, f, across)
@@ -384,8 +406,8 @@
         return remote(near[f].at[REACH + 2 * sigma], near[f].at[REACH + sigma], relay_sem, f, partner)
 
     def residual(f):
-        d_copy(f).wait_recv()
-        q_copy(f).wait_recv()
+        pl.when(has_ahead)(lambda: d_copy(f).wait_recv())
+        pl.when(has_behind)(lambda: q_copy(f).wait_recv())
 
         def rows_of(r, n):
             rows = pl.ds(r, n)
@@ -395,8 +417,8 @@
             near[f][REACH, rows, :] = res.astype(BF16)
 
         over_rows(rows_of)
-        ru_copy(f).start()
-        rd_copy(f).start()
+        pl.when(has_ahead)(lambda: ru_copy(f).start())
+        pl.when(has_behind)(lambda: rd_copy(f).start())
         rp_copy(f).start()
 
     def basis_table(fq, carry):
@@ -444,9 +466,13 @@
         return remote(e_ref.at[s, f], e_ref.at[s, f], e_sem, f, twin)
 
     def backward(f, between):
-        ru_copy(f).wait_recv()
         rp_copy(f).wait_recv()
-        relay_copy(f).wait_recv()
+
+        @pl.when(has_behind)
+        def _():
+            ru_copy(f).wait_recv()
+            relay_copy(f).wait_recv()
+
 
         def pull(q, carry):
             at = jnp.clip(inter[f, 0, q, t] - t + REACH, 0, WINDOW - 1)
@@ -530,24 +556,32 @@
         over_rows(rows_of)
 
     def relay(f):
-        rd_copy(f).wait_recv()
-        relay_copy(f).start()
+        @pl.when(has_ahead)
+        def _():
+            rd_copy(f).wait_recv()
+            relay_copy(f).start()
 
     def start_forward(f, between):
         loads[f][1].wait()
         loads[f][2].wait()
         forward(f, between)
         p_copy(f).start()
-        d_copy(f).start()
+        pl.when(has_behind)(lambda: d_copy(f).start())
 
     def nothing():
         pass
+
+    def between_first():
+        inter_in.wait()
+        count_in.wait()
+        prec_in.wait()
+        psf_move.wait()
 
     def between_last():
         merge(1)
         twin_sample(0)
 
-    start_forward(0, nothing)
+    start_forward(0, between_first)
     start_forward(1, lambda: merge(0))
     start_forward(2, between_last)
     for copy in late:
@@ -573,8 +607,20 @@
     final(2)
 
     for f in range(filters):
-        for copy in (noise_copy, p_copy, d_copy, q_copy, g_copy, ru_copy, rd_copy, rp_copy, relay_copy, e_copy):
+        for copy in (noise_copy, p_copy, g_copy, rp_copy, e_copy):
             copy(f).wait_send()
+
+    @pl.when(has_ahead)
+    def _():
+        for f in range(filters):
+            for copy in (q_copy, ru_copy, relay_copy):
+                copy(f).wait_send()
+
+    @pl.when(has_behind)
+    def _():
+        for f in range(filters):
+            for copy in (d_copy, rd_copy):
+                copy(f).wait_send()
 
 
 def body(tiles, sky_mean, sky_log_scale, noise_draw, observed, inv_var, intersections, counts, kernels, psf_coeffs, prior_prec):

time: 51.9 us -> 41.2 us (0.79); the launches traced: 51.8 us -> 40.5 us
  Pallas kernels: 49.4 us -> 38.1 us
    pallas_call x1, Pallas kernels: 49.4 us -> 38.1 us  [body(): pl.pallas_call(functools.partial(kernel, tiles), out_shape=[jax.ShapeDtyp...]
where the time goes in v5:
time: 41.2 us; the launch traced here: 40.5 us
  Pallas kernels  38.1 us (92%)
  local copies, waits for them, and re-layouts  1.76 us (4%)
  between operations  0.64 us (2%)
    pallas_call x1, Pallas kernels, body(): pl.pallas_call(functools.partial(kernel, tiles), out_shape=[jax.ShapeDtyp...  38.1 us
    unnamed x2, local copies, waits for them, and re-layouts  1.76 us

profile of v5, /device:TPU:1, one launch (start us, length us, event | category | flops | bytes accessed | tf_op | source)
XLA Modules:
  0.0 40.5 jit_solution(9052310991027928312)
XLA Ops:
  0.6 38.1 %shard_map.113 = (f32[3,256,256]{2,1,0:T(8,128)S(1)}, f32[3,256,256]{2,1,0:T(8,128)S(1)}) custom-call(f32[8,2,25]{2,1,0:T(2,128)} %kern_hbm.1, s32[6,9,3,128]{3,2,1,0:T(4,128)} %bitcast.17, s32[6,128]{1,0:T(8,128)} %bitcast.19, bf16[6,6,3,128]{3,2,1,0:T(4,128)(2,1)} %bitcast.18, f32[6,6]{1,0:T(8,128)} %prec_hbm.1, f32[3,256,256]{2,1,0:T(8,128)} %bitcast.12, ...), custom_call_target="tpu_custom_call" | custom-call | tf_op jit(solution)/shard_map/pallas_call | solution.py:636
  38.7 0.9 %copy.14 = f32[1,3,256,256]{3,2,1,0:T(8,128)} copy(f32[1,3,256,256]{3,2,1,0:T(8,128)S(1)} %bitcast.11) | data formatting | bytes 1572864
  39.6 0.9 %copy.15 = f32[1,3,256,256]{3,2,1,0:T(8,128)} copy(f32[1,3,256,256]{3,2,1,0:T(8,128)S(1)} %bitcast.10) | data formatting | bytes 1572864
